TPU v7x, 32 devices: a whole 2x2x4 slice. The times are simulated.
32 devices in a mesh: group: 2 (over y), space: 4 (over x, core), src: 4 (over z).
Axes of the slice: x: 2, y: 2, z: 4, core: 2. Of those that a mesh axis runs over, the one named last changes fastest.
Arguments:
- conductivity: float32 [128, 32, 128], P(('group', 'space')), parts along dimension 0, may hold values from 0.2 to 5
- prior_potential: float32 [8, 64, 32, 128], P(('group', 'src'), 'space'), parts along dimension 0, may hold values from -6 to 6
- electrodes: int32 [8, 2], P(('group', 'src')), parts along dimension 0, may hold values from 0 to 262143
- currents: float32 [8], P(('group', 'src')), parts along dimension 0, may hold values from 2 to 20
- receivers: int32 [512], P('group'), parts along dimension 0, may hold values from 0 to 262143
- observed: float32 [8, 256], P(('group', 'src')), parts along dimension 0, may hold values from -3 to 3
Outputs:
- potential: float32 [8, 64, 32, 128], P(('group', 'src'), 'space'), parts along dimension 0
- misfit: float32 [8, 256], P(('group', 'src')), parts along dimension 0
- gradient: float32 [128, 32, 128], P(('group', 'space')), parts along dimension 0
There are 2 independent parts, one for each index of `group`. A program takes and returns all parts, laid end to end along the dimension named above; each array names one. Nothing has to cross between parts.
Inputs may be any that keep to these rules, and one draw needn't show every extreme that they name: Flat cell indices x * 32 * 128 + y * 128 + z; a source's two electrodes may fall in any cells. Flat cell indices as for electrodes; two receivers may share a cell.
All inputs are finite; a program needn't handle non-finite values.
Results may differ from a plain program's by a relative error of at most 0.0003.
Values sent between devices are 32-bit elements; how exact they have to be, the bound alone decides.
No kernel may reach another device: no remote copies, remote signals or barrier semaphores. Data moves between devices by JAX's collectives and lax.ppermute only.
A program may use at most 128 MiB of HBM per device.

v0:
```python
import jax
import jax.numpy as jnp
from jax import lax
from jax.sharding import PartitionSpec as P

LEVELS = 4
COARSE_SWEEPS = 4


OFFSETS = ((1, 0, 0), (-1, 0, 0), (0, 1, 0), (0, -1, 0), (0, 0, 1), (0, 0, -1))


def padded_2(block, sides, width):
    for axis, dim in sides:
        count = lax.axis_size(axis)
        forward = [(i, i + 1) for i in range(count - 1)]
        backward = [(target, source) for source, target in forward]
        low = lax.ppermute(
            lax.slice_in_dim(block, block.shape[dim] - width, None, axis=dim), axis, forward
        )
        high = lax.ppermute(lax.slice_in_dim(block, 0, width, axis=dim), axis, backward)
        block = jnp.concatenate([low, block, high], axis=dim)
    return block


def shifted(array, step):
    size_x, size_y, size_z = array.shape[-3:]
    return array[
        ...,
        1 + step[0] : size_x - 1 + step[0],
        1 + step[1] : size_y - 1 + step[1],
        1 + step[2] : size_z - 1 + step[2],
    ]


def couplings(sigma_ext, weight):
    padded = jnp.pad(sigma_ext, ((0, 0), (1, 1), (1, 1)))
    centre = shifted(padded, (0, 0, 0))
    return [weight * 0.5 * (centre + shifted(padded, step)) for step in OFFSETS]


def diagonal_of(coupled):
    summed = coupled[0]
    for coupling in coupled[1:]:
        summed = summed + coupling
    return summed


def neighbours(field_ext, coupled):
    padded = jnp.pad(field_ext, ((0, 0), (0, 0), (1, 1), (1, 1)))
    summed = coupled[0] * shifted(padded, OFFSETS[0])
    for coupling, step in zip(coupled[1:], OFFSETS[1:]):
        summed = summed + coupling * shifted(padded, step)
    return summed


def relax(field_ext, right_side, coupled, diagonal, colour_mask):
    update = (right_side + neighbours(field_ext, coupled)) / diagonal
    return jnp.where(colour_mask, update, field_ext[:, 1:-1])


def parity(planes, cells_y, cells_z, first_plane):
    plane_x = first_plane + lax.iota(jnp.int32, planes)
    plane_y = lax.iota(jnp.int32, cells_y)
    plane_z = lax.iota(jnp.int32, cells_z)
    summed = plane_x[:, None, None] + plane_y[None, :, None] + plane_z[None, None, :]
    return summed % 2 == 0


def boundary_planes(field_now, width):
    return padded_2(field_now, (("space", 1),), width)


def coarsen(array):
    size_x, size_y, size_z = array.shape[-3:]
    leading = array.shape[:-3]
    blocks = array.reshape(leading + (size_x // 2, 2, size_y // 2, 2, size_z // 2, 2))
    return blocks.mean(axis=(-5, -3, -1))


def refine(array):
    return jnp.repeat(jnp.repeat(jnp.repeat(array, 2, axis=-3), 2, axis=-2), 2, axis=-1)


def pairing(forward_ext, adjoint_ext):
    forward_mid = shifted(forward_ext, (0, 0, 0))
    adjoint_mid = shifted(adjoint_ext, (0, 0, 0))
    summed = jnp.zeros(forward_mid.shape, jnp.float32)
    for step in OFFSETS:
        summed = summed + (forward_mid - shifted(forward_ext, step)) * (
            adjoint_mid - shifted(adjoint_ext, step)
        )
    return -0.5 * jnp.sum(summed, axis=0)


def sweep_plain(field_now, right_side, grid_level, from_zero, extend):
    coupled, diagonal, red_mask = (grid_level[0], grid_level[1], grid_level[2])
    if from_zero:
        field_now = jnp.where(red_mask, right_side / diagonal, 0.0)
    else:
        field_now = relax(extend(field_now, 1), right_side, coupled, diagonal, red_mask)
    return relax(extend(field_now, 1), right_side, coupled, diagonal, jnp.logical_not(red_mask))


def smooth(field_now, right_side, grid_level, from_zero):
    return sweep_plain(field_now, right_side, grid_level, from_zero, boundary_planes)


def residual_of(field_now, right_side, grid_level):
    coupled, diagonal = (grid_level[0], grid_level[1])
    return right_side - (diagonal * field_now - neighbours(boundary_planes(field_now, 1), coupled))


def cycle(levels, level_index, right_side, field_now, from_zero):
    grid_level = levels[level_index]
    if level_index == len(levels) - 1:
        for sweep_index in range(COARSE_SWEEPS):
            field_now = smooth(field_now, right_side, grid_level, sweep_index == 0)
        return field_now
    field_now = smooth(field_now, right_side, grid_level, from_zero)
    coarse_rhs = coarsen(residual_of(field_now, right_side, grid_level))
    correction = cycle(levels, level_index + 1, coarse_rhs, None, True)
    field_now = field_now + refine(correction)
    return smooth(field_now, right_side, grid_level, False)


def body(conductivity, prior_potential, electrodes, currents, receivers, observed):
    rim_width = 1
    position = lax.axis_index("space")
    levels = []
    sigma_level = conductivity
    for level_index in range(LEVELS):
        planes, cells_y, cells_z = sigma_level.shape
        weight = 0.25**level_index
        extended = boundary_planes(sigma_level[None], rim_width)[0]
        coupled_all = couplings(extended, weight)
        red_mask = parity(planes, cells_y, cells_z, position * planes)
        levels.append((coupled_all, diagonal_of(coupled_all), red_mask, None, None, None))
        if level_index < LEVELS - 1:
            sigma_level = coarsen(sigma_level)
    sources, planes, cells_y, cells_z = prior_potential.shape
    cell_count = planes * cells_y * cells_z
    offset = position * cell_count

    def placed(flat_index):
        local_index = flat_index - offset
        return jnp.where((local_index >= 0) & (local_index < cell_count), local_index, cell_count)

    source_rows = jnp.arange(sources, dtype=jnp.int32)
    source = jnp.zeros((sources, cell_count), jnp.float32)
    source = source.at[source_rows, placed(electrodes[:, 0])].add(currents, mode="drop")
    source = source.at[source_rows, placed(electrodes[:, 1])].add(-currents, mode="drop")
    source = source.reshape(sources, planes, cells_y, cells_z)
    potential = cycle(levels, 0, source, prior_potential, False)
    local_index = receivers - offset
    inside_mask = (local_index >= 0) & (local_index < cell_count)
    picked = jnp.take(
        potential.reshape(sources, cell_count), jnp.clip(local_index, 0, cell_count - 1), axis=1
    )
    partial_values = jnp.where(inside_mask[None, :], picked, 0.0)
    at_receivers = lax.psum(partial_values, "space")
    misfit = at_receivers - observed
    adjoint_source = (
        jnp.zeros((sources, cell_count), jnp.float32)
        .at[:, placed(receivers)]
        .add(misfit, mode="drop")
    )
    adjoint = cycle(
        levels, 0, adjoint_source.reshape(sources, planes, cells_y, cells_z), None, True
    )
    stacked = boundary_planes(jnp.concatenate((potential, adjoint), 0), 1)
    stacked = jnp.pad(stacked, ((0, 0), (0, 0), (1, 1), (1, 1)))
    local_terms = pairing(stacked[:sources], stacked[sources:])
    gradient = lax.psum(local_terms, "src")
    return (potential, misfit, gradient)


def solution(mesh):
    return jax.shard_map(
        body,
        mesh=mesh,
        in_specs=(
            P(("group", "space"), None, None),
            P(("group", "src"), "space", None, None),
            P(("group", "src"), None),
            P(("group", "src")),
            P("group"),
            P(("group", "src"), None),
        ),
        out_specs=(
            P(("group", "src"), "space", None, None),
            P(("group", "src"), None),
            P(("group", "space"), None, None),
        ),
        check_vma=False,
    )
```

profile of v0, /device:TPU:0, one launch (start us, length us, event | category | flops | bytes accessed | tf_op | source)
XLA Modules:
  0.0 483.4 jit_solution(1726280062933962700)
XLA Ops:
  12.3 5.1 %collective-permute-start.3 = (f32[1,1,32,128]{3,2,1,0:T(8,128)S(1)}, f32[1,1,32,128]{3,2,1,0:T(8,128)S(1)}, u32[]{:S(2)}, u32[]{:S(2)}) collective-permute-start(f32[1,1,32,128]{3,2,1,0:T(8,128)S(1)} %get-tuple-element.78), channel_id=1, source_target_pairs={{0,4},{4,8},{8,12},{1,5},{5,9},{9,13},{2,6},{6,10},{10,14},{3,7},{... | collective-permute-start | bytes 49160 | tf_op jit(solution)/shard_map/ppermute | solution.py:18
  18.8 18.9 %reshape.630 = f32[8,2,16,2,64,2]{5,4,3,2,1,0:T(8,128)} reshape(f32[16,32,128]{2,1,0:T(8,128)} %param.10) | data formatting | bytes 524288 | tf_op jit(solution)/shard_map/reshape | solution.py:77
  37.6 7.0 %reduce_sum.86 = f32[8,16,64]{2,1,0:T(8,128)S(1)} reduce(f32[8,2,16,2,64,2]{5,4,3,2,1,0:T(8,128)} %reshape.630, f32[]{:T(128)} %constant.147.clone.1), dimensions={1,3,5}, to_apply=%region_3.4 | reduce | flops 57344 | bytes 294916 | tf_op jit(solution)/shard_map/reduce_sum | solution.py:78
  56.8 5.0 %collective-permute-start.9 = (f32[1,1,16,64]{3,2,1,0:T(8,128)S(1)}, f32[1,1,16,64]{3,2,1,0:T(8,128)S(1)}, u32[]{:S(2)}, u32[]{:S(2)}) collective-permute-start(f32[1,1,16,64]{3,2,1,0:T(8,128)S(1)} %get-tuple-element.99), channel_id=1, source_target_pairs={{0,4},{4,8},{8,12},{1,5},{5,9},{9,13},{2,6},{6,10},{10,14},{3,7},{... | collective-permute-start | bytes 12296 | tf_op jit(solution)/shard_map/ppermute | solution.py:18
  64.0 4.3 collective-permute-start.5
  69.7 4.3 collective-permute-start.15
  76.0 4.3 collective-permute-start.7
  85.3 18.1 %reshape.629 = f32[8,2,16,2,64,2]{5,4,3,2,1,0:T(8,128)} reshape(f32[1,16,32,128]{3,2,1,0:T(8,128)S(1)} %fusion.94) | data formatting | bytes 524288 | tf_op jit(solution)/shard_map/reshape | solution.py:77
  103.4 7.0 %reduce_sum.85 = f32[8,16,64]{2,1,0:T(8,128)S(1)} reduce(f32[8,2,16,2,64,2]{5,4,3,2,1,0:T(8,128)} %reshape.629, f32[]{:T(128)} %constant.147.clone.1), dimensions={1,3,5}, to_apply=%region_2.3 | reduce | flops 57344 | bytes 294916 | tf_op jit(solution)/shard_map/reduce_sum | solution.py:78
  110.6 4.4 collective-permute-start.11
  131.6 3.8 collective-permute-start.17
  146.2 3.8 collective-permute-start.23
  202.8 3.8 collective-permute-start.39
  210.4 3.8 collective-permute-start.41
  217.6 3.9 collective-permute-start.43
  229.2 3.8 collective-permute-start.45
  236.9 3.9 collective-permute-start.47
  246.5 7.7 %psum.14 = f32[1,256]{1,0:T(1,128)S(1)} all-reduce(f32[1,256]{1,0:T(1,128)S(1)} %bitcast.510), channel_id=1, replica_groups=mesh['group'=2,'space'=4,'src'=4] {'space'}, use_global_device_ids=true, to_apply=%region_8.9 | all-reduce | flops 256 | bytes 2048 | tf_op jit(solution)/shard_map/psum | solution.py:161
  263.4 4.4 collective-permute-start.51
  271.6 18.1 %reshape.636 = f32[8,2,16,2,64,2]{5,4,3,2,1,0:T(8,128)} reshape(f32[1,16,32,128]{3,2,1,0:T(8,128)S(1)} %fusion.55) | data formatting | bytes 524288 | tf_op jit(solution)/shard_map/reshape | solution.py:77
  289.7 7.0 %reduce_sum.91 = f32[8,16,64]{2,1,0:T(8,128)S(1)} reduce(f32[8,2,16,2,64,2]{5,4,3,2,1,0:T(8,128)} %reshape.636, f32[]{:T(128)} %constant.147.clone.1), dimensions={1,3,5}, to_apply=%region_10.11 | reduce | flops 57344 | bytes 294916 | tf_op jit(solution)/shard_map/reduce_sum | solution.py:78
  296.9 3.9 collective-permute-start.53
  304.1 3.8 collective-permute-start.55
  316.8 3.8 collective-permute-start.57
  331.5 3.8 collective-permute-start.61
  388.1 3.8 collective-permute-start.77
  395.5 3.8 collective-permute-start.79
  402.7 3.9 collective-permute-start.81
  413.1 3.8 collective-permute-start.83
  420.7 3.9 collective-permute-start.85
  428.5 3.9 collective-permute-start.87
  437.2 37.6 %all-reduce.46.cloned.1.call-done = f32[16,32,128]{2,1,0:T(8,128)} async-done(((f32[16,32,128]{2,1,0:T(8,128)}), f32[16,32,128]{2,1,0:T(8,128)}) %all-reduce.46.cloned.1.call-update) | async-done | bytes 262160 | tf_op jit(solution)/shard_map/psum | solution.py:174
  (461 shorter events, 243.5 us)
Async XLA Ops:
  7.2 467.7 %all-reduce.46.cloned.1.call-start = ((), (), s32[]{:S(2)}) async-start(), calls=%async_computation | async-start | bytes 524288 | tf_op jit(solution)/shard_map/psum | solution.py:174
  8.0 48.8 %collective-permute-start.2 = (f32[1,1,32,128]{3,2,1,0:T(8,128)S(1)}, f32[1,1,32,128]{3,2,1,0:T(8,128)S(1)}, u32[]{:S(2)}, u32[]{:S(2)}) collective-permute-start(f32[1,1,32,128]{3,2,1,0:T(8,128)S(1)} %get-tuple-element.76), channel_id=1, source_target_pairs={{0,4},{4,8},{8,12},{1,5},{5,9},{9,13},{2,6},{6,10},{10,14},{3,7},{... | collective-permute-start | bytes 49160 | tf_op jit(solution)/shard_map/ppermute | solution.py:18
  10.3 51.5 %collective-permute-start = (f32[1,1,32,128]{3,2,1,0:T(8,128)S(1)}, f32[1,1,32,128]{3,2,1,0:T(8,128)S(1)}, u32[]{:S(2)}, u32[]{:S(2)}) collective-permute-start(f32[1,1,32,128]{3,2,1,0:T(8,128)S(1)} %get-tuple-element.77), channel_id=1, source_target_pairs={{4,0},{8,4},{12,8},{5,1},{9,5},{13,9},{6,2},{10,6},{14,10},{7,3},{... | collective-permute-start | bytes 49160 | tf_op jit(solution)/shard_map/ppermute | solution.py:21
  12.3 50.8 %collective-permute-start.3 = (f32[1,1,32,128]{3,2,1,0:T(8,128)S(1)}, f32[1,1,32,128]{3,2,1,0:T(8,128)S(1)}, u32[]{:S(2)}, u32[]{:S(2)}) collective-permute-start(f32[1,1,32,128]{3,2,1,0:T(8,128)S(1)} %get-tuple-element.78), channel_id=1, source_target_pairs={{0,4},{4,8},{8,12},{1,5},{5,9},{9,13},{2,6},{6,10},{10,14},{3,7},{... | collective-permute-start | bytes 49160 | tf_op jit(solution)/shard_map/ppermute | solution.py:18
  17.5 45.6 %collective-permute-start.1 = (f32[1,1,32,128]{3,2,1,0:T(8,128)S(1)}, f32[1,1,32,128]{3,2,1,0:T(8,128)S(1)}, u32[]{:S(2)}, u32[]{:S(2)}) collective-permute-start(f32[1,1,32,128]{3,2,1,0:T(8,128)S(1)} %get-tuple-element.79), channel_id=1, source_target_pairs={{4,0},{8,4},{12,8},{5,1},{9,5},{13,9},{6,2},{10,6},{14,10},{7,3},{... | collective-permute-start | bytes 49160 | tf_op jit(solution)/shard_map/ppermute | solution.py:21
  44.7 31.3 %collective-permute-start.8 = (f32[1,1,16,64]{3,2,1,0:T(8,128)S(1)}, f32[1,1,16,64]{3,2,1,0:T(8,128)S(1)}, u32[]{:S(2)}, u32[]{:S(2)}) collective-permute-start(f32[1,1,16,64]{3,2,1,0:T(8,128)S(1)} %get-tuple-element.98), channel_id=1, source_target_pairs={{4,0},{8,4},{12,8},{5,1},{9,5},{13,9},{6,2},{10,6},{14,10},{7,3},{... | collective-permute-start | bytes 12296 | tf_op jit(solution)/shard_map/ppermute | solution.py:21
  56.8 23.5 %collective-permute-start.9 = (f32[1,1,16,64]{3,2,1,0:T(8,128)S(1)}, f32[1,1,16,64]{3,2,1,0:T(8,128)S(1)}, u32[]{:S(2)}, u32[]{:S(2)}) collective-permute-start(f32[1,1,16,64]{3,2,1,0:T(8,128)S(1)} %get-tuple-element.99), channel_id=1, source_target_pairs={{0,4},{4,8},{8,12},{1,5},{5,9},{9,13},{2,6},{6,10},{10,14},{3,7},{... | collective-permute-start | bytes 12296 | tf_op jit(solution)/shard_map/ppermute | solution.py:18
  61.8 61.1 %collective-permute-start.14 = (f32[1,1,8,32]{3,2,1,0:T(8,128)}, f32[1,1,8,32]{3,2,1,0:T(8,128)S(1)}, u32[]{:S(2)}, u32[]{:S(2)}) collective-permute-start(f32[1,1,8,32]{3,2,1,0:T(8,128)} %get-tuple-element.118), channel_id=1, source_target_pairs={{4,0},{8,4},{12,8},{5,1},{9,5},{13,9},{6,2},{10,6},{14,10},{7,3},{... | collective-permute-start | bytes 3080 | tf_op jit(solution)/shard_map/ppermute | solution.py:21
  64.0 5.7 %collective-permute-start.5 = (f32[1,1,32,128]{3,2,1,0:T(8,128)S(1)}, f32[1,1,32,128]{3,2,1,0:T(8,128)S(1)}, u32[]{:S(2)}, u32[]{:S(2)}) collective-permute-start(f32[1,1,32,128]{3,2,1,0:T(8,128)S(1)} %get-tuple-element.74), channel_id=1, source_target_pairs={{0,4},{4,8},{8,12},{1,5},{5,9},{9,13},{2,6},{6,10},{10,14},{3,7},{... | collective-permute-start | bytes 49160 | tf_op jit(solution)/shard_map/ppermute | solution.py:18
  68.3 5.6 %collective-permute-start.4 = (f32[1,1,32,128]{3,2,1,0:T(8,128)S(1)}, f32[1,1,32,128]{3,2,1,0:T(8,128)S(1)}, u32[]{:S(2)}, u32[]{:S(2)}) collective-permute-start(f32[1,1,32,128]{3,2,1,0:T(8,128)S(1)} %get-tuple-element.75), channel_id=1, source_target_pairs={{4,0},{8,4},{12,8},{5,1},{9,5},{13,9},{6,2},{10,6},{14,10},{7,3},{... | collective-permute-start | bytes 49160 | tf_op jit(solution)/shard_map/ppermute | solution.py:21
  69.7 54.7 %collective-permute-start.15 = (f32[1,1,8,32]{3,2,1,0:T(8,128)}, f32[1,1,8,32]{3,2,1,0:T(8,128)S(1)}, u32[]{:S(2)}, u32[]{:S(2)}) collective-permute-start(f32[1,1,8,32]{3,2,1,0:T(8,128)} %get-tuple-element.119), channel_id=1, source_target_pairs={{0,4},{4,8},{8,12},{1,5},{5,9},{9,13},{2,6},{6,10},{10,14},{3,7},{... | collective-permute-start | bytes 3080 | tf_op jit(solution)/shard_map/ppermute | solution.py:18
  74.0 69.9 %collective-permute-start.20 = (f32[1,1,4,16]{3,2,1,0:T(4,128)}, f32[1,1,4,16]{3,2,1,0:T(4,128)S(1)}, u32[]{:S(2)}, u32[]{:S(2)}) collective-permute-start(f32[1,1,4,16]{3,2,1,0:T(4,128)} %get-tuple-element.148), channel_id=1, source_target_pairs={{4,0},{8,4},{12,8},{5,1},{9,5},{13,9},{6,2},{10,6},{14,10},{7,3},{... | collective-permute-start | bytes 776 | tf_op jit(solution)/shard_map/ppermute | solution.py:21
  76.0 5.6 %collective-permute-start.7 = (f32[1,1,32,128]{3,2,1,0:T(8,128)S(1)}, f32[1,1,32,128]{3,2,1,0:T(8,128)S(1)}, u32[]{:S(2)}, u32[]{:S(2)}) collective-permute-start(f32[1,1,32,128]{3,2,1,0:T(8,128)S(1)} %get-tuple-element.72), channel_id=1, source_target_pairs={{0,4},{4,8},{8,12},{1,5},{5,9},{9,13},{2,6},{6,10},{10,14},{3,7},{... | collective-permute-start | bytes 49160 | tf_op jit(solution)/shard_map/ppermute | solution.py:18
  110.6 5.7 %collective-permute-start.11 = (f32[1,1,16,64]{3,2,1,0:T(8,128)S(1)}, f32[1,1,16,64]{3,2,1,0:T(8,128)S(1)}, u32[]{:S(2)}, u32[]{:S(2)}) collective-permute-start(f32[1,1,16,64]{3,2,1,0:T(8,128)S(1)} %get-tuple-element.96), channel_id=1, source_target_pairs={{0,4},{4,8},{8,12},{1,5},{5,9},{9,13},{2,6},{6,10},{10,14},{3,7},{... | collective-permute-start | bytes 12296 | tf_op jit(solution)/shard_map/ppermute | solution.py:18
  116.3 27.5 %collective-permute-start.21 = (f32[1,1,4,16]{3,2,1,0:T(4,128)S(1)}, f32[1,1,4,16]{3,2,1,0:T(4,128)S(1)}, u32[]{:S(2)}, u32[]{:S(2)}) collective-permute-start(f32[1,1,4,16]{3,2,1,0:T(4,128)S(1)} %copy-done.45), channel_id=1, source_target_pairs={{0,4},{4,8},{8,12},{1,5},{5,9},{9,13},{2,6},{6,10},{10,14},{3,7},{... | collective-permute-start | bytes 776 | tf_op jit(solution)/shard_map/ppermute | solution.py:18
  131.6 5.2 %collective-permute-start.17 = (f32[1,1,8,32]{3,2,1,0:T(8,128)S(1)}, f32[1,1,8,32]{3,2,1,0:T(8,128)S(1)}, u32[]{:S(2)}, u32[]{:S(2)}) collective-permute-start(f32[1,1,8,32]{3,2,1,0:T(8,128)S(1)} %get-tuple-element.116), channel_id=1, source_target_pairs={{0,4},{4,8},{8,12},{1,5},{5,9},{9,13},{2,6},{6,10},{10,14},{3,7},{... | collective-permute-start | bytes 3080 | tf_op jit(solution)/shard_map/ppermute | solution.py:18
  138.7 5.2 %collective-permute-start.19 = (f32[1,1,8,32]{3,2,1,0:T(8,128)S(1)}, f32[1,1,8,32]{3,2,1,0:T(8,128)S(1)}, u32[]{:S(2)}, u32[]{:S(2)}) collective-permute-start(f32[1,1,8,32]{3,2,1,0:T(8,128)S(1)} %get-tuple-element.114), channel_id=1, source_target_pairs={{0,4},{4,8},{8,12},{1,5},{5,9},{9,13},{2,6},{6,10},{10,14},{3,7},{... | collective-permute-start | bytes 3080 | tf_op jit(solution)/shard_map/ppermute | solution.py:18
  146.2 5.1 %collective-permute-start.23 = (f32[1,1,4,16]{3,2,1,0:T(4,128)S(1)}, f32[1,1,4,16]{3,2,1,0:T(4,128)S(1)}, u32[]{:S(2)}, u32[]{:S(2)}) collective-permute-start(f32[1,1,4,16]{3,2,1,0:T(4,128)S(1)} %get-tuple-element.146), channel_id=1, source_target_pairs={{0,4},{4,8},{8,12},{1,5},{5,9},{9,13},{2,6},{6,10},{10,14},{3,7},{... | collective-permute-start | bytes 776 | tf_op jit(solution)/shard_map/ppermute | solution.py:18
  202.8 5.1 %collective-permute-start.39 = (f32[1,1,8,32]{3,2,1,0:T(8,128)S(1)}, f32[1,1,8,32]{3,2,1,0:T(8,128)S(1)}, u32[]{:S(2)}, u32[]{:S(2)}) collective-permute-start(f32[1,1,8,32]{3,2,1,0:T(8,128)S(1)} %get-tuple-element.108), channel_id=1, source_target_pairs={{0,4},{4,8},{8,12},{1,5},{5,9},{9,13},{2,6},{6,10},{10,14},{3,7},{... | collective-permute-start | bytes 3080 | tf_op jit(solution)/shard_map/ppermute | solution.py:18
  217.6 5.2 %collective-permute-start.43 = (f32[1,1,16,64]{3,2,1,0:T(8,128)S(1)}, f32[1,1,16,64]{3,2,1,0:T(8,128)S(1)}, u32[]{:S(2)}, u32[]{:S(2)}) collective-permute-start(f32[1,1,16,64]{3,2,1,0:T(8,128)S(1)} %get-tuple-element.88), channel_id=1, source_target_pairs={{0,4},{4,8},{8,12},{1,5},{5,9},{9,13},{2,6},{6,10},{10,14},{3,7},{... | collective-permute-start | bytes 12296 | tf_op jit(solution)/shard_map/ppermute | solution.py:18
  229.2 5.8 %collective-permute-start.45 = (f32[1,1,32,128]{3,2,1,0:T(8,128)S(1)}, f32[1,1,32,128]{3,2,1,0:T(8,128)S(1)}, u32[]{:S(2)}, u32[]{:S(2)}) collective-permute-start(f32[1,1,32,128]{3,2,1,0:T(8,128)S(1)} %get-tuple-element.70), channel_id=1, source_target_pairs={{0,4},{4,8},{8,12},{1,5},{5,9},{9,13},{2,6},{6,10},{10,14},{3,7},{... | collective-permute-start | bytes 49160 | tf_op jit(solution)/shard_map/ppermute | solution.py:18
  236.9 5.2 %collective-permute-start.47 = (f32[1,1,32,128]{3,2,1,0:T(8,128)S(1)}, f32[1,1,32,128]{3,2,1,0:T(8,128)S(1)}, u32[]{:S(2)}, u32[]{:S(2)}) collective-permute-start(f32[1,1,32,128]{3,2,1,0:T(8,128)S(1)} %get-tuple-element.68), channel_id=1, source_target_pairs={{0,4},{4,8},{8,12},{1,5},{5,9},{9,13},{2,6},{6,10},{10,14},{3,7},{... | collective-permute-start | bytes 49160 | tf_op jit(solution)/shard_map/ppermute | solution.py:18
  263.4 5.9 %collective-permute-start.51 = (f32[1,1,32,128]{3,2,1,0:T(8,128)S(1)}, f32[1,1,32,128]{3,2,1,0:T(8,128)S(1)}, u32[]{:S(2)}, u32[]{:S(2)}) collective-permute-start(f32[1,1,32,128]{3,2,1,0:T(8,128)S(1)} %get-tuple-element.64), channel_id=1, source_target_pairs={{0,4},{4,8},{8,12},{1,5},{5,9},{9,13},{2,6},{6,10},{10,14},{3,7},{... | collective-permute-start | bytes 49160 | tf_op jit(solution)/shard_map/ppermute | solution.py:18
  296.9 5.2 %collective-permute-start.53 = (f32[1,1,16,64]{3,2,1,0:T(8,128)S(1)}, f32[1,1,16,64]{3,2,1,0:T(8,128)S(1)}, u32[]{:S(2)}, u32[]{:S(2)}) collective-permute-start(f32[1,1,16,64]{3,2,1,0:T(8,128)S(1)} %get-tuple-element.86), channel_id=1, source_target_pairs={{0,4},{4,8},{8,12},{1,5},{5,9},{9,13},{2,6},{6,10},{10,14},{3,7},{... | collective-permute-start | bytes 12296 | tf_op jit(solution)/shard_map/ppermute | solution.py:18
  304.1 5.1 %collective-permute-start.55 = (f32[1,1,16,64]{3,2,1,0:T(8,128)S(1)}, f32[1,1,16,64]{3,2,1,0:T(8,128)S(1)}, u32[]{:S(2)}, u32[]{:S(2)}) collective-permute-start(f32[1,1,16,64]{3,2,1,0:T(8,128)S(1)} %get-tuple-element.84), channel_id=1, source_target_pairs={{0,4},{4,8},{8,12},{1,5},{5,9},{9,13},{2,6},{6,10},{10,14},{3,7},{... | collective-permute-start | bytes 12296 | tf_op jit(solution)/shard_map/ppermute | solution.py:18
  316.8 5.2 %collective-permute-start.57 = (f32[1,1,8,32]{3,2,1,0:T(8,128)S(1)}, f32[1,1,8,32]{3,2,1,0:T(8,128)S(1)}, u32[]{:S(2)}, u32[]{:S(2)}) collective-permute-start(f32[1,1,8,32]{3,2,1,0:T(8,128)S(1)} %get-tuple-element.106), channel_id=1, source_target_pairs={{0,4},{4,8},{8,12},{1,5},{5,9},{9,13},{2,6},{6,10},{10,14},{3,7},{... | collective-permute-start | bytes 3080 | tf_op jit(solution)/shard_map/ppermute | solution.py:18
  331.5 5.1 %collective-permute-start.61 = (f32[1,1,4,16]{3,2,1,0:T(4,128)S(1)}, f32[1,1,4,16]{3,2,1,0:T(4,128)S(1)}, u32[]{:S(2)}, u32[]{:S(2)}) collective-permute-start(f32[1,1,4,16]{3,2,1,0:T(4,128)S(1)} %get-tuple-element.132), channel_id=1, source_target_pairs={{0,4},{4,8},{8,12},{1,5},{5,9},{9,13},{2,6},{6,10},{10,14},{3,7},{... | collective-permute-start | bytes 776 | tf_op jit(solution)/shard_map/ppermute | solution.py:18
  388.1 5.1 %collective-permute-start.77 = (f32[1,1,8,32]{3,2,1,0:T(8,128)S(1)}, f32[1,1,8,32]{3,2,1,0:T(8,128)S(1)}, u32[]{:S(2)}, u32[]{:S(2)}) collective-permute-start(f32[1,1,8,32]{3,2,1,0:T(8,128)S(1)} %get-tuple-element.100), channel_id=1, source_target_pairs={{0,4},{4,8},{8,12},{1,5},{5,9},{9,13},{2,6},{6,10},{10,14},{3,7},{... | collective-permute-start | bytes 3080 | tf_op jit(solution)/shard_map/ppermute | solution.py:18
  402.7 5.2 %collective-permute-start.81 = (f32[1,1,16,64]{3,2,1,0:T(8,128)S(1)}, f32[1,1,16,64]{3,2,1,0:T(8,128)S(1)}, u32[]{:S(2)}, u32[]{:S(2)}) collective-permute-start(f32[1,1,16,64]{3,2,1,0:T(8,128)S(1)} %get-tuple-element.80), channel_id=1, source_target_pairs={{0,4},{4,8},{8,12},{1,5},{5,9},{9,13},{2,6},{6,10},{10,14},{3,7},{... | collective-permute-start | bytes 12296 | tf_op jit(solution)/shard_map/ppermute | solution.py:18
  413.1 5.2 %collective-permute-start.83 = (f32[1,1,32,128]{3,2,1,0:T(8,128)S(1)}, f32[1,1,32,128]{3,2,1,0:T(8,128)S(1)}, u32[]{:S(2)}, u32[]{:S(2)}) collective-permute-start(f32[1,1,32,128]{3,2,1,0:T(8,128)S(1)} %get-tuple-element.62), channel_id=1, source_target_pairs={{0,4},{4,8},{8,12},{1,5},{5,9},{9,13},{2,6},{6,10},{10,14},{3,7},{... | collective-permute-start | bytes 49160 | tf_op jit(solution)/shard_map/ppermute | solution.py:18
  420.7 5.2 %collective-permute-start.85 = (f32[1,1,32,128]{3,2,1,0:T(8,128)S(1)}, f32[1,1,32,128]{3,2,1,0:T(8,128)S(1)}, u32[]{:S(2)}, u32[]{:S(2)}) collective-permute-start(f32[1,1,32,128]{3,2,1,0:T(8,128)S(1)} %get-tuple-element.60), channel_id=1, source_target_pairs={{0,4},{4,8},{8,12},{1,5},{5,9},{9,13},{2,6},{6,10},{10,14},{3,7},{... | collective-permute-start | bytes 49160 | tf_op jit(solution)/shard_map/ppermute | solution.py:18
  428.5 5.2 %collective-permute-start.87 = (f32[2,1,32,128]{3,2,1,0:T(8,128)S(1)}, f32[2,1,32,128]{3,2,1,0:T(8,128)S(1)}, u32[]{:S(2)}, u32[]{:S(2)}) collective-permute-start(f32[2,1,32,128]{3,2,1,0:T(8,128)S(1)} %get-tuple-element.58), channel_id=1, source_target_pairs={{0,4},{4,8},{8,12},{1,5},{5,9},{9,13},{2,6},{6,10},{10,14},{3,7},{... | collective-permute-start | bytes 98312 | tf_op jit(solution)/shard_map/ppermute | solution.py:18
  (105 other events, 2470.0 us)
Sparse Core Ops, SparseCore 0:
  437.4 37.4 all-reduce.45
where the time goes:
time: 486 us; the launch traced here: 483 us
  starting transfers between devices  225 us (46%)
  waiting for transfers between devices  104 us (21%)
  local copies, waits for them, and re-layouts  79.3 us (16%)
  other arithmetic  45.4 us (9%)
  between operations  21.3 us (4%)
  blocking collectives  7.67 us (2%)
    ppermute x44, starting transfers between devices, padded_2(): lax.ppermute(lax.slice_in_dim(block, block.shape[dim] - width, None, axis...  168 us
    ppermute x44, waiting for transfers between devices, padded_2(): lax.ppermute(lax.slice_in_dim(block, 0, width, axis=dim), axis, backward)  66.6 us
    reshape x7, local copies, waits for them, and re-layouts, coarsen(): array.reshape(leading + (size_x // 2, 2, size_y // 2, 2, size_z // 2, 2))  62.3 us
    ppermute x44, starting transfers between devices, padded_2(): lax.ppermute(lax.slice_in_dim(block, 0, width, axis=dim), axis, backward)  57.3 us
    psum x1, waiting for transfers between devices, body(): gradient = lax.psum(local_terms, 'src')  37.6 us
    reduce_sum x9, other arithmetic, coarsen(): return blocks.mean(axis=(-5, -3, -1))  25.2 us
  transfers between devices with their start and end apart: 89, of which 38 were waited for; matrix products, arithmetic and copies ran while one was open for 14% of the time, Pallas kernels for 0%

commit v1 on v0

v1 whole, which is shorter than its diff:
```python
import functools

import jax
import jax.numpy as jnp
from jax import lax
from jax.experimental import pallas as pl
from jax.experimental.pallas import tpu as pltpu
from jax.sharding import PartitionSpec as P

LEVELS = 4
COARSE_SWEEPS = 4
SUB = 8
LANES = 128
ROWS = (4, 2, 1, 1)
Y_STEP = (1, 1, 1, 2)
UNROLL = (4, 4, 8, 8)


class Level:
    def __init__(self, index, planes, field, right, couple_x, couple_y, couple_z, diagonal, inverse, sigma):
        self.index, self.planes = index, planes
        self.rows, self.y_step, self.z_step = ROWS[index], Y_STEP[index], 1 << index
        self.field, self.right = field, right
        self.couple_x, self.couple_y, self.couple_z = couple_x, couple_y, couple_z
        self.diagonal, self.inverse, self.sigma = diagonal, inverse, sigma
        self.unroll = min(UNROLL[index], planes)
        lane = lax.broadcasted_iota(jnp.int32, (SUB, LANES), 1)
        sub = lax.broadcasted_iota(jnp.int32, (SUB, LANES), 0)
        self.lane, self.sub = lane, sub
        parity = (lane >> index) & 1
        if index == 2:
            parity = (parity + sub) & 1
        if index == 3:
            parity = (parity + (sub >> 1)) & 1
        self.even = parity == 0
        self.odd = parity == 1
        self.z_even = ((lane >> index) & 1) == 0
        self.last_z = lane >= LANES - self.z_step
        self.last_y = sub >= SUB - self.y_step
        self.first_z = lane < self.z_step
        self.first_y = sub < self.y_step

    def mask(self, plane, row, colour):
        return self.even if (plane + row + colour) % 2 == 0 else self.odd

    def z_up(self, value):
        return pltpu.roll(value, LANES - self.z_step, 1)

    def z_down(self, value):
        return pltpu.roll(value, self.z_step, 1)

    def y_up(self, value):
        return pltpu.roll(value, SUB - self.y_step, 0)

    def y_down(self, value):
        return pltpu.roll(value, self.y_step, 0)


def blocks(level, body, start=None, stop=None):
    count = level.planes // level.unroll
    if start is None and count == 1:
        body(0)
        return
    first = 0 if start is None else start // level.unroll
    last = count if stop is None else stop // level.unroll

    def step(block, carry):
        body(block * level.unroll)
        return carry

    lax.fori_loop(first, last, step, 0)


def setup(level):
    rows = level.rows

    def body(base):
        sig = [[level.sigma[base + p, j] for j in range(rows)] for p in range(level.unroll + 2)]
        for p in range(level.unroll):
            for j in range(rows):
                mid = sig[p + 1][j]
                above = mid + sig[p + 2][j]
                below = mid + sig[p][j]
                if j + 1 < rows:
                    y_above = sig[p + 1][j + 1]
                else:
                    y_above = jnp.where(level.last_y, 0.0, level.y_up(sig[p + 1][0]))
                if j > 0:
                    y_below = sig[p + 1][j - 1]
                else:
                    y_below = jnp.where(level.first_y, 0.0, level.y_down(sig[p + 1][rows - 1]))
                z_above = jnp.where(level.last_z, 0.0, level.z_up(mid))
                z_below = jnp.where(level.first_z, 0.0, level.z_down(mid))
                diagonal = above + below + (4.0 * mid + ((y_above + y_below) + (z_above + z_below)))
                level.couple_x[base + p + 1, j] = above
                if j + 1 < rows:
                    level.couple_y[base + p, j] = mid + y_above
                else:
                    level.couple_y[base + p, j] = jnp.where(level.last_y, 0.0, mid + y_above)
                level.couple_z[base + p, j] = jnp.where(level.last_z, 0.0, mid + z_above)
                level.diagonal[base + p, j] = diagonal
                level.inverse[base + p, j] = 1.0 / diagonal

    for j in range(rows):
        level.couple_x[0, j] = jnp.zeros((SUB, LANES), jnp.float32)
    blocks(level, body)


def gathered(level, field, base):
    rows = level.rows
    planes = [[field[base + p, j] for j in range(rows)] for p in range(level.unroll + 2)]
    couple_x = [[level.couple_x[base + p, j] for j in range(rows)] for p in range(level.unroll + 1)]
    sums = []
    for p in range(level.unroll):
        mid = planes[p + 1]
        couple_y = [level.couple_y[base + p, j] for j in range(rows)]
        row = []
        for j in range(rows):
            couple_z = level.couple_z[base + p, j]
            total = level.right[base + p, j] + couple_x[p + 1][j] * planes[p + 2][j]
            total = total + couple_x[p][j] * planes[p][j]
            y_above = mid[j + 1] if j + 1 < rows else level.y_up(mid[0])
            total = total + couple_y[j] * y_above
            if j > 0:
                total = total + couple_y[j - 1] * mid[j - 1]
            else:
                total = total + level.y_down(couple_y[rows - 1] * mid[rows - 1])
            total = total + (couple_z * level.z_up(mid[j]) + level.z_down(couple_z * mid[j]))
            row.append(total)
        sums.append(row)
    return sums, planes


def half_sweep(level, field, colour, start=None, stop=None):
    def body(base):
        sums, planes = gathered(level, field, base)
        for p in range(level.unroll):
            for j in range(level.rows):
                update = sums[p][j] * level.inverse[base + p, j]
                field[base + p + 1, j] = jnp.where(level.mask(p, j, colour), update, planes[p + 1][j])

    blocks(level, body, start, stop)


def red_from_zero(level, field):
    def body(base):
        for p in range(level.unroll):
            for j in range(level.rows):
                update = level.right[base + p, j] * level.inverse[base + p, j]
                field[base + p + 1, j] = jnp.where(level.mask(p, j, 0), update, 0.0)

    blocks(level, body)


def summed_pairs(level, low, high):
    both = [a + b for a, b in zip(low, high)]
    if level.rows > 1:
        both = [both[j] + both[j + 1] for j in range(0, level.rows, 2)]
    else:
        both = [v + jnp.where((level.sub & 1) == 0, level.y_up(v), level.y_down(v)) for v in both]
    return [v + jnp.where(level.z_even, level.z_up(v), level.z_down(v)) for v in both]


def restrict_residual(level, field, coarse):
    def body(base):
        sums, planes = gathered(level, field, base)
        left = [
            [sums[p][j] - level.diagonal[base + p, j] * planes[p + 1][j] for j in range(level.rows)]
            for p in range(level.unroll)
        ]
        for p in range(0, level.unroll, 2):
            for j, value in enumerate(summed_pairs(level, left[p], left[p + 1])):
                coarse.right[base // 2 + p // 2, j] = 0.5 * value

    blocks(level, body)


def restrict_sigma(level, coarse):
    def body(base):
        for p in range(0, level.unroll, 2):
            low = [level.sigma[base + p + 1, j] for j in range(level.rows)]
            high = [level.sigma[base + p + 2, j] for j in range(level.rows)]
            for j, value in enumerate(summed_pairs(level, low, high)):
                coarse.sigma[base // 2 + p // 2 + 1, j] = 0.125 * value

    blocks(level, body)


def correct(level, field, coarse, start=None, stop=None):
    def body(base):
        for p in range(level.unroll):
            for j in range(level.rows):
                e = coarse.field[base // 2 + p // 2 + 1, j * coarse.rows // level.rows]
                field[base + p + 1, j] = field[base + p + 1, j] + e

    blocks(level, body, start, stop)


def coarse_solve(levels, index):
    level = levels[index]
    if index == len(levels) - 1:
        red_from_zero(level, level.field)
        half_sweep(level, level.field, 1)
        for _ in range(COARSE_SWEEPS - 1):
            half_sweep(level, level.field, 0)
            half_sweep(level, level.field, 1)
        return
    red_from_zero(level, level.field)
    half_sweep(level, level.field, 1)
    restrict_residual(level, level.field, levels[index + 1])
    coarse_solve(levels, index + 1)
    correct(level, level.field, levels[index + 1])
    half_sweep(level, level.field, 0)
    half_sweep(level, level.field, 1)


def cell_of(flat):
    y = (flat >> 7) & 31
    return flat >> 12, y & 3, y >> 2, flat & 127


def kernel(masks, total, ints, currents, observed, *refs):
    parts = len(masks)
    sigma_parts, prior_parts = refs[:parts], refs[parts : 2 * parts]
    potential_out, misfit_out, keep_out, send_out = refs[2 * parts : 2 * parts + 4]
    scratch = list(refs[2 * parts + 4 :])
    forward = scratch.pop(0)
    local = prior_parts[0].shape[1]
    levels = []
    for index in range(LEVELS):
        arrays = [scratch.pop(0) for _ in range(7)]
        sigma = scratch.pop(0) if index else arrays[0]
        levels.append(Level(index, total >> index, *arrays, sigma))
    fine = levels[0]
    adjoint = fine.field
    position, half = ints[0], ints[1]
    receivers = ints.shape[0] - 4
    zero = jnp.zeros((SUB, LANES), jnp.float32)

    for level in levels:
        for ref in [level.field] + ([level.sigma] if level.index else [forward]):
            for j in range(level.rows):
                ref[0, j] = zero
                ref[level.planes + 1, j] = zero

    for mask, sigma_part, prior_part in zip(masks, sigma_parts, prior_parts):
        base = (position ^ mask) * local

        def place(plane, carry, base=base, sigma_part=sigma_part, prior_part=prior_part):
            for j in range(ROWS[0]):
                adjoint[base + plane + 1, j] = sigma_part[plane, pl.ds(j, SUB, stride=4), :]
                forward[base + plane + 1, j] = prior_part[0, plane, pl.ds(j, SUB, stride=4), :]
                fine.right[base + plane, j] = zero
            return carry

        lax.fori_loop(0, local, place, 0, unroll=2)

    setup(fine)
    for index in range(LEVELS - 1):
        restrict_sigma(levels[index], levels[index + 1])
        setup(levels[index + 1])
    for j in range(ROWS[0]):
        adjoint[0, j] = zero
        adjoint[fine.planes + 1, j] = zero

    lane = lax.broadcasted_iota(jnp.int32, (1, LANES), 1)
    for which, sign in ((0, 2.0), (1, -2.0)):
        x, j, s, z = cell_of(ints[2 + which])
        row = fine.right[x, j, pl.ds(s, 1), :]
        fine.right[x, j, pl.ds(s, 1), :] = row + jnp.where(lane == z, sign * currents[0], 0.0)

    half_sweep(fine, forward, 0)
    half_sweep(fine, forward, 1)
    restrict_residual(fine, forward, levels[1])
    coarse_solve(levels, 1)
    correct(fine, forward, levels[1])
    half_sweep(fine, forward, 0)
    half_sweep(fine, forward, 1)

    for which in range(2):
        x, j, s, z = cell_of(ints[2 + which])
        fine.right[x, j, pl.ds(s, 1), :] = jnp.zeros((1, LANES), jnp.float32)

    def receive(k, carry):
        x, j, s, z = cell_of(ints[4 + k])
        value = jnp.where(lane == z, forward[x + 1, j, pl.ds(s, 1), :] - observed[k], 0.0)
        misfit_out[pl.ds(k, 1), :] = value
        fine.right[x, j, pl.ds(s, 1), :] = fine.right[x, j, pl.ds(s, 1), :] + 2.0 * value
        return carry

    lax.fori_loop(0, receivers, receive, 0, unroll=4)

    first = position * local
    margin = fine.unroll
    low = jnp.maximum(first - margin, 0)
    high = jnp.minimum(first + local + margin, fine.planes)
    red_from_zero(fine, adjoint)
    half_sweep(fine, adjoint, 1)
    restrict_residual(fine, adjoint, levels[1])
    coarse_solve(levels, 1)
    correct(fine, adjoint, levels[1], jnp.maximum(low - margin, 0), jnp.minimum(high + margin, fine.planes))
    half_sweep(fine, adjoint, 0, low, high)
    half_sweep(fine, adjoint, 1, low, high)

    def gradient(base, out, out_base):
        def plane_of(plane, carry):
            at = base + plane + 1
            p = [forward[at, j] for j in range(4)]
            a = [adjoint[at, j] for j in range(4)]
            y_pairs = []
            for j in range(4):
                if j < 3:
                    up_p, up_a = p[j + 1], a[j + 1]
                else:
                    up_p = jnp.where(fine.last_y, 0.0, fine.y_up(p[0]))
                    up_a = jnp.where(fine.last_y, 0.0, fine.y_up(a[0]))
                y_pairs.append((p[j] - up_p) * (a[j] - up_a))
            for j in range(4):
                own = p[j] * a[j]
                value = (p[j] - forward[at - 1, j]) * (a[j] - adjoint[at - 1, j])
                value = value + (p[j] - forward[at + 1, j]) * (a[j] - adjoint[at + 1, j])
                if j > 0:
                    y_below = y_pairs[j - 1]
                else:
                    y_below = jnp.where(fine.first_y, own, fine.y_down(y_pairs[3]))
                value = value + (y_pairs[j] + y_below)
                up_p = jnp.where(fine.last_z, 0.0, fine.z_up(p[j]))
                up_a = jnp.where(fine.last_z, 0.0, fine.z_up(a[j]))
                z_pair = (p[j] - up_p) * (a[j] - up_a)
                z_below = jnp.where(fine.first_z, own, fine.z_down(z_pair))
                value = value + (z_pair + z_below)
                out[out_base + plane, pl.ds(j, SUB, stride=4), :] = -0.5 * value
            return carry

        lax.fori_loop(0, local // 2, plane_of, 0, unroll=2)

    def deliver(plane, carry):
        for j in range(4):
            potential_out[0, plane, pl.ds(j, SUB, stride=4), :] = forward[first + plane + 1, j]
        return carry

    gradient(first + half * (local // 2), keep_out, 0)
    gradient(first + (1 - half) * (local // 2), send_out, 0)
    lax.fori_loop(0, local, deliver, 0, unroll=2)


def solve(sigma_parts, prior_parts, masks, ints, currents, observed):
    local, cells_y, cells_z = sigma_parts[0].shape
    parts = len(masks)
    total = local * parts
    receivers = observed.shape[-1]

    def planes(count, index):
        return pltpu.VMEM((count, ROWS[index], SUB, LANES), jnp.float32)

    scratch = [planes(total + 2, 0)]
    for index in range(LEVELS):
        n = total >> index
        scratch += [planes(n + 2, index), planes(n, index), planes(n + 1, index)]
        scratch += [planes(n, index) for _ in range(4)]
        if index:
            scratch.append(planes(n + 2, index))
    held = 4 * sum(s.shape[0] * s.shape[1] * SUB * LANES for s in scratch)
    held += 4 * cells_y * cells_z * local * (2 * parts + 2) + 4 * LANES * receivers
    half = jax.ShapeDtypeStruct((local // 2, cells_y, cells_z), jnp.float32)
    smem = pl.BlockSpec(memory_space=pltpu.SMEM)
    vmem = pl.BlockSpec(memory_space=pltpu.VMEM)
    return pl.pallas_call(
        functools.partial(kernel, masks, total),
        out_shape=(
            jax.ShapeDtypeStruct((1, local, cells_y, cells_z), jnp.float32),
            jax.ShapeDtypeStruct((receivers, LANES), jnp.float32),
            half,
            half,
        ),
        in_specs=[smem] * 3 + [vmem] * (2 * parts),
        out_specs=[vmem] * 4,
        scratch_shapes=scratch,
        compiler_params=pltpu.CompilerParams(vmem_limit_bytes=min(held + (6 << 20), 63 << 20)),
        name="both_cycles",
    )(ints, currents, observed, *sigma_parts, *prior_parts)


def exchanged(value, axis, mask):
    return lax.ppermute(value, axis, [(i, i ^ mask) for i in range(lax.axis_size(axis))])


def body(conductivity, prior_potential, electrodes, currents, receivers, observed):
    count = lax.axis_size("space")
    position = lax.axis_index("space")
    source = lax.axis_index("src")
    sigma_parts, prior_parts, masks = [conductivity], [prior_potential], [0]
    bit = count // 2
    while bit:
        sigma_parts += [exchanged(part, "space", bit) for part in sigma_parts]
        prior_parts += [exchanged(part, "space", bit) for part in prior_parts]
        masks += [mask ^ bit for mask in masks]
        bit //= 2
    upper = source & 1
    ints = jnp.concatenate([jnp.stack([position, upper]), electrodes[0], receivers])
    potential, picked, keep, send = solve(
        sigma_parts, prior_parts, tuple(masks), ints, currents, observed[0]
    )
    misfit = jnp.sum(picked, axis=1)[None, :]
    summed = keep + exchanged(send, "src", 1)
    bit = 2
    while bit < lax.axis_size("src"):
        summed = summed + exchanged(summed, "src", bit)
        bit *= 2
    other = exchanged(summed, "src", 1)
    gradient = jnp.concatenate(
        [jnp.where(upper == 1, other, summed), jnp.where(upper == 1, summed, other)], 0
    )
    return potential, misfit, gradient


def solution(mesh):
    return jax.shard_map(
        body,
        mesh=mesh,
        in_specs=(
            P(("group", "space"), None, None),
            P(("group", "src"), "space", None, None),
            P(("group", "src"), None),
            P(("group", "src")),
            P("group"),
            P(("group", "src"), None),
        ),
        out_specs=(
            P(("group", "src"), "space", None, None),
            P(("group", "src"), None),
            P(("group", "space"), None, None),
        ),
        check_vma=False,
    )
```

time: 486 us -> 76.5 us (0.16)
  starting transfers between devices: 225 us -> 9.03 us
  waiting for transfers between devices: 104 us -> 26 us
  local copies, waits for them, and re-layouts: 79.3 us -> 3.13 us
  other arithmetic: 45.4 us -> 1.53 us
  Pallas kernels: 0 us -> 35.3 us
  between operations: 21.3 us -> 1.34 us
  blocking collectives: 7.67 us -> 0 us
    ppermute x88 -> x9, starting transfers between devices: 225 us -> 9.03 us  [exchanged(): lax.ppermute(value, axis, [(i, i ^ mask) for i in range(lax.axis_size(axi...]
    reshape x7 -> x0, local copies, waits for them, and re-layouts: 62.3 us -> none  [coarsen(): array.reshape(leading + (size_x // 2, 2, size_y // 2, 2, size_z // 2, 2))]
    ppermute x88 -> x9, waiting for transfers between devices: 66.7 us -> 26 us  [exchanged(): lax.ppermute(value, axis, [(i, i ^ mask) for i in range(lax.axis_size(axi...]
    psum x1 -> x0, waiting for transfers between devices: 37.6 us -> none  [body(): gradient = lax.psum(local_terms, 'src')]
    pallas_call x0 -> x1, Pallas kernels: none -> 35.3 us  [solve(): pl.pallas_call(functools.partial(kernel, masks, total), out_shape=(jax.Sh...]
    reduce_sum x9 -> x1, other arithmetic: 25.2 us -> 0.67 us  [body(): misfit = jnp.sum(picked, axis=1)[None, :]]
    psum x1 -> x0, blocking collectives: 7.67 us -> none  [body(): at_receivers = lax.psum(partial_values, 'space')]
    select_n x42 -> x1, other arithmetic: 7.56 us -> 0.02 us  [body(): jnp.where(upper == 1, other, summed)]
  transfers between devices with their start and end apart: 89 -> 9, of which waited for: 38 -> 6; matrix products, arithmetic and copies ran while one was open for 14% -> 1% of each run, Pallas kernels for 0% -> 0%
where the time goes in v1:
time: 76.5 us; the launch traced here: 76.3 us
  Pallas kernels  35.3 us (46%)
  waiting for transfers between devices  26 us (34%)
  starting transfers between devices  9.03 us (12%)
  local copies, waits for them, and re-layouts  3.13 us (4%)
  other arithmetic  1.53 us (2%)
  between operations  1.34 us (2%)
    pallas_call x1, Pallas kernels, solve(): pl.pallas_call(functools.partial(kernel, masks, total), out_shape=(jax.Sh...  35.3 us
    ppermute x9, waiting for transfers between devices, exchanged(): lax.ppermute(value, axis, [(i, i ^ mask) for i in range(lax.axis_size(axi...  26 us
    ppermute x9, starting transfers between devices, exchanged(): lax.ppermute(value, axis, [(i, i ^ mask) for i in range(lax.axis_size(axi...  9.03 us
    unnamed x10, local copies, waits for them, and re-layouts  3.13 us
  transfers between devices with their start and end apart: 9, of which 6 were waited for; matrix products, arithmetic and copies ran while one was open for 1% of the time, Pallas kernels for 0%

profile of v1, /device:TPU:0, one launch (start us, length us, event | category | flops | bytes accessed | tf_op | source)
XLA Modules:
  0.0 76.3 jit_solution(16585701055766816387)
XLA Ops:
  0.6 3.0 %collective-permute-start = (f32[16,32,128]{2,1,0:T(8,128)}, f32[16,32,128]{2,1,0:T(8,128)S(1)}, u32[]{:S(2)}, u32[]{:S(2)}) collective-permute-start(f32[16,32,128]{2,1,0:T(8,128)} %refs_0_.1), channel_id=1, source_target_pairs={{0,8},{4,12},{8,0},{12,4},{1,9},{5,13},{9,1},{13,5},{2,10},{6,14},... | collective-permute-start | bytes 786440 | tf_op jit(solution)/shard_map/ppermute | solution.py:385
  3.6 0.1 collective-permute-start.3
  3.7 0.0 collective-permute-start.1
  3.7 0.5 collective-permute-start.4
  4.2 6.8 %collective-permute-done.refs_1_ = f32[16,32,128]{2,1,0:T(8,128)S(1)} collective-permute-done((f32[16,32,128]{2,1,0:T(8,128)}, f32[16,32,128]{2,1,0:T(8,128)S(1)}, u32[]{:S(2)}, u32[]{:S(2)}) %collective-permute-start) | collective-permute-done | bytes 262176 | tf_op jit(solution)/shard_map/ppermute | solution.py:385
  11.0 0.0 collective-permute-start.2
  11.0 4.8 %collective-permute-done.3.refs_5_ = f32[1,16,32,128]{3,2,1,0:T(8,128)S(1)} collective-permute-done((f32[1,16,32,128]{3,2,1,0:T(8,128)}, f32[1,16,32,128]{3,2,1,0:T(8,128)S(1)}, u32[]{:S(2)}, u32[]{:S(2)}) %collective-permute-start.3) | collective-permute-done | bytes 262176 | tf_op jit(solution)/shard_map/ppermute | solution.py:385
  15.8 0.0 collective-permute-start.5
  16.4 0.0 copy-start.3
  16.4 0.0 copy-start.4
  16.4 0.7 copy-done.3
  17.1 0.0 copy-done.4
  17.1 0.1 pad_add_fusion.ints
  17.2 0.0 copy-start.2
  17.2 0.0 collective-permute-done.1.refs_2_
  17.2 0.0 collective-permute-done.4.refs_6_
  17.2 0.0 collective-permute-done.2.refs_3_
  17.2 0.1 collective-permute-done.5.refs_7_
  17.3 0.6 copy-done.2
  17.9 0.0 copy-start
  17.9 0.9 %copy-done = f32[16,32,128]{2,1,0:T(8,128)S(1)} copy-done((f32[16,32,128]{2,1,0:T(8,128)S(1)}, f32[16,32,128]{2,1,0:T(8,128)}, u32[]{:S(2)}) %copy-start) | copy-done | bytes 262168
  18.8 0.0 copy-start.1
  18.8 0.9 %copy-done.1 = f32[1,16,32,128]{3,2,1,0:T(8,128)S(1)} copy-done((f32[1,16,32,128]{3,2,1,0:T(8,128)S(1)}, f32[1,16,32,128]{3,2,1,0:T(8,128)}, u32[]{:S(2)}) %copy-start.1) | copy-done | bytes 262168
  19.8 35.3 %both_cycles.1 = (f32[1,16,32,128]{3,2,1,0:T(8,128)}, f32[256,128]{1,0:T(8,128)S(1)}, f32[8,32,128]{2,1,0:T(8,128)S(1)}, f32[8,32,128]{2,1,0:T(8,128)S(1)}) custom-call(s32[260]{0:T(512)S(1)} %pad_add_fusion.ints, f32[1]{0:T(128)S(6)} %copy.9.currents, f32[256]{0:T(256)S(1)} %bitcast.5, f32[16,32,128]{2,1,0:T(8,128)S(1)} %copy-done, ...), custom_call_target="tpu_custom_call" | custom-call | tf_op jit(solution)/shard_map/both_cycles/pallas_call | solution.py:368
  55.1 1.8 %collective-permute-start.6 = (f32[8,32,128]{2,1,0:T(8,128)S(1)}, f32[8,32,128]{2,1,0:T(8,128)S(1)}, u32[]{:S(2)}, u32[]{:S(2)}) collective-permute-start(f32[8,32,128]{2,1,0:T(8,128)S(1)} %get-tuple-element.10), channel_id=1, source_target_pairs={{0,1},{1,0},{2,3},{3,2},{4,5},{5,4},{6,7},{7,6},{8,9},{9,8},{10,11... | collective-permute-start | bytes 393224 | tf_op jit(solution)/shard_map/ppermute | solution.py:385
  56.9 4.4 %collective-permute-done.6 = f32[8,32,128]{2,1,0:T(8,128)S(1)} collective-permute-done((f32[8,32,128]{2,1,0:T(8,128)S(1)}, f32[8,32,128]{2,1,0:T(8,128)S(1)}, u32[]{:S(2)}, u32[]{:S(2)}) %collective-permute-start.6) | collective-permute-done | bytes 131104 | tf_op jit(solution)/shard_map/ppermute | solution.py:385
  61.3 2.8 %collective-permute-start.7 = (f32[8,32,128]{2,1,0:T(8,128)S(1)}, f32[8,32,128]{2,1,0:T(8,128)S(1)}, u32[]{:S(2)}, u32[]{:S(2)}) collective-permute-start(f32[8,32,128]{2,1,0:T(8,128)S(1)} %add.6), channel_id=1, source_target_pairs={{0,2},{1,3},{2,0},{3,1},{4,6},{5,7},{6,4},{7,5},{8,10},{9,11},{10,... | collective-permute-start | bytes 393224 | tf_op jit(solution)/shard_map/ppermute | solution.py:385
  64.2 6.4 %collective-permute-done.7 = f32[8,32,128]{2,1,0:T(8,128)S(1)} collective-permute-done((f32[8,32,128]{2,1,0:T(8,128)S(1)}, f32[8,32,128]{2,1,0:T(8,128)S(1)}, u32[]{:S(2)}, u32[]{:S(2)}) %collective-permute-start.7) | collective-permute-done | bytes 131104 | tf_op jit(solution)/shard_map/ppermute | solution.py:385
  70.5 0.8 %collective-permute-start.8 = (f32[8,32,128]{2,1,0:T(8,128)S(1)}, f32[8,32,128]{2,1,0:T(8,128)S(1)}, u32[]{:S(2)}, u32[]{:S(2)}) collective-permute-start(f32[8,32,128]{2,1,0:T(8,128)S(1)} %add.7), channel_id=1, source_target_pairs={{0,1},{1,0},{2,3},{3,2},{4,5},{5,4},{6,7},{7,6},{8,9},{9,8},{10,11... | collective-permute-start | bytes 393224 | tf_op jit(solution)/shard_map/ppermute | solution.py:385
  71.3 0.7 reduce_sum.9
  72.0 3.6 %collective-permute-done.8 = f32[8,32,128]{2,1,0:T(8,128)S(1)} collective-permute-done((f32[8,32,128]{2,1,0:T(8,128)S(1)}, f32[8,32,128]{2,1,0:T(8,128)S(1)}, u32[]{:S(2)}, u32[]{:S(2)}) %collective-permute-start.8) | collective-permute-done | bytes 131104 | tf_op jit(solution)/shard_map/ppermute | solution.py:385
  75.6 0.7 pad_maximum_fusion
  (3 shorter events, 0.1 us)
Async XLA Ops:
  0.6 10.4 %collective-permute-start = (f32[16,32,128]{2,1,0:T(8,128)}, f32[16,32,128]{2,1,0:T(8,128)S(1)}, u32[]{:S(2)}, u32[]{:S(2)}) collective-permute-start(f32[16,32,128]{2,1,0:T(8,128)} %refs_0_.1), channel_id=1, source_target_pairs={{0,8},{4,12},{8,0},{12,4},{1,9},{5,13},{9,1},{13,5},{2,10},{6,14},... | collective-permute-start | bytes 786440 | tf_op jit(solution)/shard_map/ppermute | solution.py:385
  3.6 12.1 %collective-permute-start.3 = (f32[1,16,32,128]{3,2,1,0:T(8,128)}, f32[1,16,32,128]{3,2,1,0:T(8,128)S(1)}, u32[]{:S(2)}, u32[]{:S(2)}) collective-permute-start(f32[1,16,32,128]{3,2,1,0:T(8,128)} %refs_4_.1), channel_id=1, source_target_pairs={{0,8},{4,12},{8,0},{12,4},{1,9},{5,13},{9,1},{13,5},{2,10},{6,14},... | collective-permute-start | bytes 786440 | tf_op jit(solution)/shard_map/ppermute | solution.py:385
  3.7 13.5 %collective-permute-start.1 = (f32[16,32,128]{2,1,0:T(8,128)}, f32[16,32,128]{2,1,0:T(8,128)S(1)}, u32[]{:S(2)}, u32[]{:S(2)}) collective-permute-start(f32[16,32,128]{2,1,0:T(8,128)} %refs_0_.1), channel_id=1, source_target_pairs={{0,4},{4,0},{8,12},{12,8},{1,5},{5,1},{9,13},{13,9},{2,6},{6,2},{1... | collective-permute-start | bytes 786440 | tf_op jit(solution)/shard_map/ppermute | solution.py:385
  3.7 13.5 %collective-permute-start.4 = (f32[1,16,32,128]{3,2,1,0:T(8,128)}, f32[1,16,32,128]{3,2,1,0:T(8,128)S(1)}, u32[]{:S(2)}, u32[]{:S(2)}) collective-permute-start(f32[1,16,32,128]{3,2,1,0:T(8,128)} %refs_4_.1), channel_id=1, source_target_pairs={{0,4},{4,0},{8,12},{12,8},{1,5},{5,1},{9,13},{13,9},{2,6},{6,2},{1... | collective-permute-start | bytes 786440 | tf_op jit(solution)/shard_map/ppermute | solution.py:385
  11.0 6.2 %collective-permute-start.2 = (f32[16,32,128]{2,1,0:T(8,128)S(1)}, f32[16,32,128]{2,1,0:T(8,128)S(1)}, u32[]{:S(2)}, u32[]{:S(2)}) collective-permute-start(f32[16,32,128]{2,1,0:T(8,128)S(1)} %collective-permute-done.refs_1_), channel_id=1, source_target_pairs={{0,4},{4,0},{8,12},{12,8},{1,5},{5,1},{9,13},{13,9},{2,6},{6,2},{1... | collective-permute-start | bytes 786440 | tf_op jit(solution)/shard_map/ppermute | solution.py:385
  15.8 1.5 %collective-permute-start.5 = (f32[1,16,32,128]{3,2,1,0:T(8,128)S(1)}, f32[1,16,32,128]{3,2,1,0:T(8,128)S(1)}, u32[]{:S(2)}, u32[]{:S(2)}) collective-permute-start(f32[1,16,32,128]{3,2,1,0:T(8,128)S(1)} %collective-permute-done.3.refs_5_), channel_id=1, source_target_pairs={{0,4},{4,0},{8,12},{12,8},{1,5},{5,1},{9,13},{13,9},{2,6},{6,2},{1... | collective-permute-start | bytes 786440 | tf_op jit(solution)/shard_map/ppermute | solution.py:385
  16.4 0.7 copy-start.3
  16.4 0.7 copy-start.4
  17.2 0.7 copy-start.2
  17.9 0.9 %copy-start = (f32[16,32,128]{2,1,0:T(8,128)S(1)}, f32[16,32,128]{2,1,0:T(8,128)}, u32[]{:S(2)}) copy-start(f32[16,32,128]{2,1,0:T(8,128)} %refs_0_.1) | copy-start | bytes 786436
  18.8 0.9 %copy-start.1 = (f32[1,16,32,128]{3,2,1,0:T(8,128)S(1)}, f32[1,16,32,128]{3,2,1,0:T(8,128)}, u32[]{:S(2)}) copy-start(f32[1,16,32,128]{3,2,1,0:T(8,128)} %refs_4_.1) | copy-start | bytes 786436
  55.1 6.2 %collective-permute-start.6 = (f32[8,32,128]{2,1,0:T(8,128)S(1)}, f32[8,32,128]{2,1,0:T(8,128)S(1)}, u32[]{:S(2)}, u32[]{:S(2)}) collective-permute-start(f32[8,32,128]{2,1,0:T(8,128)S(1)} %get-tuple-element.10), channel_id=1, source_target_pairs={{0,1},{1,0},{2,3},{3,2},{4,5},{5,4},{6,7},{7,6},{8,9},{9,8},{10,11... | collective-permute-start | bytes 393224 | tf_op jit(solution)/shard_map/ppermute | solution.py:385
  61.3 9.2 %collective-permute-start.7 = (f32[8,32,128]{2,1,0:T(8,128)S(1)}, f32[8,32,128]{2,1,0:T(8,128)S(1)}, u32[]{:S(2)}, u32[]{:S(2)}) collective-permute-start(f32[8,32,128]{2,1,0:T(8,128)S(1)} %add.6), channel_id=1, source_target_pairs={{0,2},{1,3},{2,0},{3,1},{4,6},{5,7},{6,4},{7,5},{8,10},{9,11},{10,... | collective-permute-start | bytes 393224 | tf_op jit(solution)/shard_map/ppermute | solution.py:385
  70.5 5.0 %collective-permute-start.8 = (f32[8,32,128]{2,1,0:T(8,128)S(1)}, f32[8,32,128]{2,1,0:T(8,128)S(1)}, u32[]{:S(2)}, u32[]{:S(2)}) collective-permute-start(f32[8,32,128]{2,1,0:T(8,128)S(1)} %add.7), channel_id=1, source_target_pairs={{0,1},{1,0},{2,3},{3,2},{4,5},{5,4},{6,7},{7,6},{8,9},{9,8},{10,11... | collective-permute-start | bytes 393224 | tf_op jit(solution)/shard_map/ppermute | solution.py:385

commit v2 on v1

--- a/solution.py
+++ b/solution.py
@@ -13,7 +13,7 @@
 LANES = 128
 ROWS = (4, 2, 1, 1)
 Y_STEP = (1, 1, 1, 2)
-UNROLL = (4, 4, 8, 8)
+UNROLL = (32, 32, 16, 8)
 
 
 class Level:
@@ -56,27 +56,28 @@
         return pltpu.roll(value, self.y_step, 0)
 
 
-def blocks(level, body, start=None, stop=None):
+def blocks(level, body, window=None):
+    if window is not None:
+        body(*window)
+        return
     count = level.planes // level.unroll
-    if start is None and count == 1:
-        body(0)
+    if count == 1:
+        body(0, level.unroll)
         return
-    first = 0 if start is None else start // level.unroll
-    last = count if stop is None else stop // level.unroll
 
     def step(block, carry):
-        body(block * level.unroll)
+        body(block * level.unroll, level.unroll)
         return carry
 
-    lax.fori_loop(first, last, step, 0)
+    lax.fori_loop(0, count, step, 0)
 
 
 def setup(level):
     rows = level.rows
 
-    def body(base):
-        sig = [[level.sigma[base + p, j] for j in range(rows)] for p in range(level.unroll + 2)]
-        for p in range(level.unroll):
+    def body(base, count):
+        sig = [[level.sigma[base + p, j] for j in range(rows)] for p in range(count + 2)]
+        for p in range(count):
             for j in range(rows):
                 mid = sig[p + 1][j]
                 above = mid + sig[p + 2][j]
@@ -106,12 +107,12 @@
     blocks(level, body)
 
 
-def gathered(level, field, base):
+def gathered(level, field, base, count):
     rows = level.rows
-    planes = [[field[base + p, j] for j in range(rows)] for p in range(level.unroll + 2)]
-    couple_x = [[level.couple_x[base + p, j] for j in range(rows)] for p in range(level.unroll + 1)]
+    planes = [[field[base + p, j] for j in range(rows)] for p in range(count + 2)]
+    couple_x = [[level.couple_x[base + p, j] for j in range(rows)] for p in range(count + 1)]
     sums = []
-    for p in range(level.unroll):
+    for p in range(count):
         mid = planes[p + 1]
         couple_y = [level.couple_y[base + p, j] for j in range(rows)]
         row = []
@@ -131,20 +132,20 @@
     return sums, planes
 
 
-def half_sweep(level, field, colour, start=None, stop=None):
-    def body(base):
-        sums, planes = gathered(level, field, base)
-        for p in range(level.unroll):
+def half_sweep(level, field, colour, window=None):
+    def body(base, count):
+        sums, planes = gathered(level, field, base, count)
+        for p in range(count):
             for j in range(level.rows):
                 update = sums[p][j] * level.inverse[base + p, j]
                 field[base + p + 1, j] = jnp.where(level.mask(p, j, colour), update, planes[p + 1][j])
 
-    blocks(level, body, start, stop)
+    blocks(level, body, window)
 
 
 def red_from_zero(level, field):
-    def body(base):
-        for p in range(level.unroll):
+    def body(base, count):
+        for p in range(count):
             for j in range(level.rows):
                 update = level.right[base + p, j] * level.inverse[base + p, j]
                 field[base + p + 1, j] = jnp.where(level.mask(p, j, 0), update, 0.0)
@@ -162,13 +163,13 @@
 
 
 def restrict_residual(level, field, coarse):
-    def body(base):
-        sums, planes = gathered(level, field, base)
+    def body(base, count):
+        sums, planes = gathered(level, field, base, count)
         left = [
             [sums[p][j] - level.diagonal[base + p, j] * planes[p + 1][j] for j in range(level.rows)]
-            for p in range(level.unroll)
+            for p in range(count)
         ]
-        for p in range(0, level.unroll, 2):
+        for p in range(0, count, 2):
             for j, value in enumerate(summed_pairs(level, left[p], left[p + 1])):
                 coarse.right[base // 2 + p // 2, j] = 0.5 * value
 
@@ -176,8 +177,8 @@
 
 
 def restrict_sigma(level, coarse):
-    def body(base):
-        for p in range(0, level.unroll, 2):
+    def body(base, count):
+        for p in range(0, count, 2):
             low = [level.sigma[base + p + 1, j] for j in range(level.rows)]
             high = [level.sigma[base + p + 2, j] for j in range(level.rows)]
             for j, value in enumerate(summed_pairs(level, low, high)):
@@ -186,14 +187,14 @@
     blocks(level, body)
 
 
-def correct(level, field, coarse, start=None, stop=None):
-    def body(base):
-        for p in range(level.unroll):
+def correct(level, field, coarse, window=None):
+    def body(base, count):
+        for p in range(count):
             for j in range(level.rows):
                 e = coarse.field[base // 2 + p // 2 + 1, j * coarse.rows // level.rows]
                 field[base + p + 1, j] = field[base + p + 1, j] + e
 
-    blocks(level, body, start, stop)
+    blocks(level, body, window)
 
 
 def coarse_solve(levels, index):
@@ -253,7 +254,7 @@
                 fine.right[base + plane, j] = zero
             return carry
 
-        lax.fori_loop(0, local, place, 0, unroll=2)
+        lax.fori_loop(0, local, place, 0, unroll=16)
 
     setup(fine)
     for index in range(LEVELS - 1):
@@ -288,19 +289,21 @@
         fine.right[x, j, pl.ds(s, 1), :] = fine.right[x, j, pl.ds(s, 1), :] + 2.0 * value
         return carry
 
-    lax.fori_loop(0, receivers, receive, 0, unroll=4)
+    lax.fori_loop(0, receivers, receive, 0, unroll=32)
 
     first = position * local
-    margin = fine.unroll
-    low = jnp.maximum(first - margin, 0)
-    high = jnp.minimum(first + local + margin, fine.planes)
+
+    def window(margin):
+        count = min(local + 2 * margin, fine.planes)
+        return jnp.clip(first - margin, 0, fine.planes - count), count
+
     red_from_zero(fine, adjoint)
     half_sweep(fine, adjoint, 1)
     restrict_residual(fine, adjoint, levels[1])
     coarse_solve(levels, 1)
-    correct(fine, adjoint, levels[1], jnp.maximum(low - margin, 0), jnp.minimum(high + margin, fine.planes))
-    half_sweep(fine, adjoint, 0, low, high)
-    half_sweep(fine, adjoint, 1, low, high)
+    correct(fine, adjoint, levels[1], window(4))
+    half_sweep(fine, adjoint, 0, window(2))
+    half_sweep(fine, adjoint, 1, window(2))
 
     def gradient(base, out, out_base):
         def plane_of(plane, carry):
@@ -332,7 +335,7 @@
                 out[out_base + plane, pl.ds(j, SUB, stride=4), :] = -0.5 * value
             return carry
 
-        lax.fori_loop(0, local // 2, plane_of, 0, unroll=2)
+        lax.fori_loop(0, local // 2, plane_of, 0, unroll=8)
 
     def deliver(plane, carry):
         for j in range(4):
@@ -341,7 +344,7 @@
 
     gradient(first + half * (local // 2), keep_out, 0)
     gradient(first + (1 - half) * (local // 2), send_out, 0)
-    lax.fori_loop(0, local, deliver, 0, unroll=2)
+    lax.fori_loop(0, local, deliver, 0, unroll=16)
 
 
 def solve(sigma_parts, prior_parts, masks, ints, currents, observed):

time: 76.5 us -> 54.3 us (0.71)
  Pallas kernels: 35.3 us -> 13.5 us
    pallas_call x1, Pallas kernels: 35.3 us -> 13.5 us  [solve(): pl.pallas_call(functools.partial(kernel, masks, total), out_shape=(jax.Sh...]
where the time goes in v2:
time: 54.3 us; the launch traced here: 54.1 us
  waiting for transfers between devices  25.6 us (47%)
  Pallas kernels  13.5 us (25%)
  starting transfers between devices  9.03 us (17%)
  local copies, waits for them, and re-layouts  3.13 us (6%)
  other arithmetic  1.53 us (3%)
  between operations  1.34 us (2%)
    ppermute x9, waiting for transfers between devices, exchanged(): lax.ppermute(value, axis, [(i, i ^ mask) for i in range(lax.axis_size(axi...  25.6 us
    pallas_call x1, Pallas kernels, solve(): pl.pallas_call(functools.partial(kernel, masks, total), out_shape=(jax.Sh...  13.5 us
    ppermute x9, starting transfers between devices, exchanged(): lax.ppermute(value, axis, [(i, i ^ mask) for i in range(lax.axis_size(axi...  9.03 us
    unnamed x10, local copies, waits for them, and re-layouts  3.13 us
  transfers between devices with their start and end apart: 9, of which 6 were waited for; matrix products, arithmetic and copies ran while one was open for 1% of the time, Pallas kernels for 0%

profile of v2, /device:TPU:0, one launch (start us, length us, event | category | flops | bytes accessed | tf_op | source)
XLA Modules:
  0.0 54.1 jit_solution(10990923345738948863)
XLA Ops:
  0.6 3.0 %collective-permute-start = (f32[16,32,128]{2,1,0:T(8,128)}, f32[16,32,128]{2,1,0:T(8,128)S(1)}, u32[]{:S(2)}, u32[]{:S(2)}) collective-permute-start(f32[16,32,128]{2,1,0:T(8,128)} %refs_0_.1), channel_id=1, source_target_pairs={{0,8},{4,12},{8,0},{12,4},{1,9},{5,13},{9,1},{13,5},{2,10},{6,14},... | collective-permute-start | bytes 786440 | tf_op jit(solution)/shard_map/ppermute | solution.py:388
  3.6 0.1 collective-permute-start.3
  3.7 0.0 collective-permute-start.1
  3.7 0.5 collective-permute-start.4
  4.2 6.8 %collective-permute-done.refs_1_ = f32[16,32,128]{2,1,0:T(8,128)S(1)} collective-permute-done((f32[16,32,128]{2,1,0:T(8,128)}, f32[16,32,128]{2,1,0:T(8,128)S(1)}, u32[]{:S(2)}, u32[]{:S(2)}) %collective-permute-start) | collective-permute-done | bytes 262176 | tf_op jit(solution)/shard_map/ppermute | solution.py:388
  11.0 0.0 collective-permute-start.2
  11.0 4.8 %collective-permute-done.3.refs_5_ = f32[1,16,32,128]{3,2,1,0:T(8,128)S(1)} collective-permute-done((f32[1,16,32,128]{3,2,1,0:T(8,128)}, f32[1,16,32,128]{3,2,1,0:T(8,128)S(1)}, u32[]{:S(2)}, u32[]{:S(2)}) %collective-permute-start.3) | collective-permute-done | bytes 262176 | tf_op jit(solution)/shard_map/ppermute | solution.py:388
  15.8 0.0 collective-permute-start.5
  16.4 0.0 copy-start.3
  16.4 0.0 copy-start.4
  16.4 0.7 %copy-done.3 = s32[256]{0:T(256)S(1)} copy-done((s32[256]{0:T(256)S(1)}, s32[256]{0:T(256)}, u32[]{:S(2)}) %copy-start.3) | copy-done | bytes 1048
  17.1 0.0 copy-done.4
  17.1 0.1 pad_add_fusion.ints
  17.2 0.0 copy-start.2
  17.2 0.0 collective-permute-done.1.refs_2_
  17.2 0.0 collective-permute-done.4.refs_6_
  17.2 0.0 collective-permute-done.2.refs_3_
  17.2 0.1 collective-permute-done.5.refs_7_
  17.3 0.6 %copy-done.2 = f32[1,256]{1,0:T(1,128)S(1)} copy-done((f32[1,256]{1,0:T(1,128)S(1)}, f32[1,256]{1,0:T(1,128)}, u32[]{:S(2)}) %copy-start.2) | copy-done | bytes 1048
  17.9 0.0 copy-start
  17.9 0.9 %copy-done = f32[16,32,128]{2,1,0:T(8,128)S(1)} copy-done((f32[16,32,128]{2,1,0:T(8,128)S(1)}, f32[16,32,128]{2,1,0:T(8,128)}, u32[]{:S(2)}) %copy-start) | copy-done | bytes 262168
  18.8 0.0 copy-start.1
  18.8 0.9 %copy-done.1 = f32[1,16,32,128]{3,2,1,0:T(8,128)S(1)} copy-done((f32[1,16,32,128]{3,2,1,0:T(8,128)S(1)}, f32[1,16,32,128]{3,2,1,0:T(8,128)}, u32[]{:S(2)}) %copy-start.1) | copy-done | bytes 262168
  19.8 13.5 %both_cycles.1 = (f32[1,16,32,128]{3,2,1,0:T(8,128)}, f32[256,128]{1,0:T(8,128)S(1)}, f32[8,32,128]{2,1,0:T(8,128)S(1)}, f32[8,32,128]{2,1,0:T(8,128)S(1)}) custom-call(s32[260]{0:T(512)S(1)} %pad_add_fusion.ints, f32[1]{0:T(128)S(6)} %copy.9.currents, f32[256]{0:T(256)S(1)} %bitcast.5, f32[16,32,128]{2,1,0:T(8,128)S(1)} %copy-done, ...), custom_call_target="tpu_custom_call" | custom-call | tf_op jit(solution)/shard_map/both_cycles/pallas_call | solution.py:371
  33.2 1.8 %collective-permute-start.6 = (f32[8,32,128]{2,1,0:T(8,128)S(1)}, f32[8,32,128]{2,1,0:T(8,128)S(1)}, u32[]{:S(2)}, u32[]{:S(2)}) collective-permute-start(f32[8,32,128]{2,1,0:T(8,128)S(1)} %get-tuple-element.10), channel_id=1, source_target_pairs={{0,1},{1,0},{2,3},{3,2},{4,5},{5,4},{6,7},{7,6},{8,9},{9,8},{10,11... | collective-permute-start | bytes 393224 | tf_op jit(solution)/shard_map/ppermute | solution.py:388
  35.1 4.2 %collective-permute-done.6 = f32[8,32,128]{2,1,0:T(8,128)S(1)} collective-permute-done((f32[8,32,128]{2,1,0:T(8,128)S(1)}, f32[8,32,128]{2,1,0:T(8,128)S(1)}, u32[]{:S(2)}, u32[]{:S(2)}) %collective-permute-start.6) | collective-permute-done | bytes 131104 | tf_op jit(solution)/shard_map/ppermute | solution.py:388
  39.2 2.8 %collective-permute-start.7 = (f32[8,32,128]{2,1,0:T(8,128)S(1)}, f32[8,32,128]{2,1,0:T(8,128)S(1)}, u32[]{:S(2)}, u32[]{:S(2)}) collective-permute-start(f32[8,32,128]{2,1,0:T(8,128)S(1)} %add.6), channel_id=1, source_target_pairs={{0,2},{1,3},{2,0},{3,1},{4,6},{5,7},{6,4},{7,5},{8,10},{9,11},{10,... | collective-permute-start | bytes 393224 | tf_op jit(solution)/shard_map/ppermute | solution.py:388
  42.1 6.2 %collective-permute-done.7 = f32[8,32,128]{2,1,0:T(8,128)S(1)} collective-permute-done((f32[8,32,128]{2,1,0:T(8,128)S(1)}, f32[8,32,128]{2,1,0:T(8,128)S(1)}, u32[]{:S(2)}, u32[]{:S(2)}) %collective-permute-start.7) | collective-permute-done | bytes 131104 | tf_op jit(solution)/shard_map/ppermute | solution.py:388
  48.3 0.8 %collective-permute-start.8 = (f32[8,32,128]{2,1,0:T(8,128)S(1)}, f32[8,32,128]{2,1,0:T(8,128)S(1)}, u32[]{:S(2)}, u32[]{:S(2)}) collective-permute-start(f32[8,32,128]{2,1,0:T(8,128)S(1)} %add.7), channel_id=1, source_target_pairs={{0,1},{1,0},{2,3},{3,2},{4,5},{5,4},{6,7},{7,6},{8,9},{9,8},{10,11... | collective-permute-start | bytes 393224 | tf_op jit(solution)/shard_map/ppermute | solution.py:388
  49.1 0.7 %reduce_sum.9 = f32[256]{0:T(256)} reduce(f32[256,128]{1,0:T(8,128)S(1)} %get-tuple-element.8, f32[]{:T(128)} %constant.10.clone.1), dimensions={1}, to_apply=%region_0.0 | reduce | flops 32512 | bytes 132100 | tf_op jit(solution)/shard_map/reduce_sum | solution.py:407
  49.8 3.6 %collective-permute-done.8 = f32[8,32,128]{2,1,0:T(8,128)S(1)} collective-permute-done((f32[8,32,128]{2,1,0:T(8,128)S(1)}, f32[8,32,128]{2,1,0:T(8,128)S(1)}, u32[]{:S(2)}, u32[]{:S(2)}) %collective-permute-start.8) | collective-permute-done | bytes 131104 | tf_op jit(solution)/shard_map/ppermute | solution.py:388
  53.3 0.7 %pad_maximum_fusion = f32[16,32,128]{2,1,0:T(8,128)} fusion(f32[8,32,128]{2,1,0:T(8,128)S(1)} %get-tuple-element.12, f32[8,32,128]{2,1,0:T(8,128)S(1)} %get-tuple-element.11), kind=kLoop, calls=%fused_computation | loop fusion | flops 65536 | bytes 524288 | tf_op jit(solution)/shard_map/concatenate | solution.py:414
  (3 shorter events, 0.1 us)
Async XLA Ops:
  0.6 10.4 %collective-permute-start = (f32[16,32,128]{2,1,0:T(8,128)}, f32[16,32,128]{2,1,0:T(8,128)S(1)}, u32[]{:S(2)}, u32[]{:S(2)}) collective-permute-start(f32[16,32,128]{2,1,0:T(8,128)} %refs_0_.1), channel_id=1, source_target_pairs={{0,8},{4,12},{8,0},{12,4},{1,9},{5,13},{9,1},{13,5},{2,10},{6,14},... | collective-permute-start | bytes 786440 | tf_op jit(solution)/shard_map/ppermute | solution.py:388
  3.6 12.1 %collective-permute-start.3 = (f32[1,16,32,128]{3,2,1,0:T(8,128)}, f32[1,16,32,128]{3,2,1,0:T(8,128)S(1)}, u32[]{:S(2)}, u32[]{:S(2)}) collective-permute-start(f32[1,16,32,128]{3,2,1,0:T(8,128)} %refs_4_.1), channel_id=1, source_target_pairs={{0,8},{4,12},{8,0},{12,4},{1,9},{5,13},{9,1},{13,5},{2,10},{6,14},... | collective-permute-start | bytes 786440 | tf_op jit(solution)/shard_map/ppermute | solution.py:388
  3.7 13.5 %collective-permute-start.1 = (f32[16,32,128]{2,1,0:T(8,128)}, f32[16,32,128]{2,1,0:T(8,128)S(1)}, u32[]{:S(2)}, u32[]{:S(2)}) collective-permute-start(f32[16,32,128]{2,1,0:T(8,128)} %refs_0_.1), channel_id=1, source_target_pairs={{0,4},{4,0},{8,12},{12,8},{1,5},{5,1},{9,13},{13,9},{2,6},{6,2},{1... | collective-permute-start | bytes 786440 | tf_op jit(solution)/shard_map/ppermute | solution.py:388
  3.7 13.5 %collective-permute-start.4 = (f32[1,16,32,128]{3,2,1,0:T(8,128)}, f32[1,16,32,128]{3,2,1,0:T(8,128)S(1)}, u32[]{:S(2)}, u32[]{:S(2)}) collective-permute-start(f32[1,16,32,128]{3,2,1,0:T(8,128)} %refs_4_.1), channel_id=1, source_target_pairs={{0,4},{4,0},{8,12},{12,8},{1,5},{5,1},{9,13},{13,9},{2,6},{6,2},{1... | collective-permute-start | bytes 786440 | tf_op jit(solution)/shard_map/ppermute | solution.py:388
  11.0 6.2 %collective-permute-start.2 = (f32[16,32,128]{2,1,0:T(8,128)S(1)}, f32[16,32,128]{2,1,0:T(8,128)S(1)}, u32[]{:S(2)}, u32[]{:S(2)}) collective-permute-start(f32[16,32,128]{2,1,0:T(8,128)S(1)} %collective-permute-done.refs_1_), channel_id=1, source_target_pairs={{0,4},{4,0},{8,12},{12,8},{1,5},{5,1},{9,13},{13,9},{2,6},{6,2},{1... | collective-permute-start | bytes 786440 | tf_op jit(solution)/shard_map/ppermute | solution.py:388
  15.8 1.5 %collective-permute-start.5 = (f32[1,16,32,128]{3,2,1,0:T(8,128)S(1)}, f32[1,16,32,128]{3,2,1,0:T(8,128)S(1)}, u32[]{:S(2)}, u32[]{:S(2)}) collective-permute-start(f32[1,16,32,128]{3,2,1,0:T(8,128)S(1)} %collective-permute-done.3.refs_5_), channel_id=1, source_target_pairs={{0,4},{4,0},{8,12},{12,8},{1,5},{5,1},{9,13},{13,9},{2,6},{6,2},{1... | collective-permute-start | bytes 786440 | tf_op jit(solution)/shard_map/ppermute | solution.py:388
  16.4 0.7 %copy-start.3 = (s32[256]{0:T(256)S(1)}, s32[256]{0:T(256)}, u32[]{:S(2)}) copy-start(s32[256]{0:T(256)} %param.10) | copy-start | bytes 3076
  16.4 0.7 %copy-start.4 = (s32[1,2]{1,0:T(1,128)S(1)}, s32[1,2]{1,0:T(1,128)}, u32[]{:S(2)}) copy-start(s32[1,2]{1,0:T(1,128)} %param.8) | copy-start | bytes 28
  17.2 0.7 %copy-start.2 = (f32[1,256]{1,0:T(1,128)S(1)}, f32[1,256]{1,0:T(1,128)}, u32[]{:S(2)}) copy-start(f32[1,256]{1,0:T(1,128)} %param.11) | copy-start | bytes 3076
  17.9 0.9 %copy-start = (f32[16,32,128]{2,1,0:T(8,128)S(1)}, f32[16,32,128]{2,1,0:T(8,128)}, u32[]{:S(2)}) copy-start(f32[16,32,128]{2,1,0:T(8,128)} %refs_0_.1) | copy-start | bytes 786436
  18.8 0.9 %copy-start.1 = (f32[1,16,32,128]{3,2,1,0:T(8,128)S(1)}, f32[1,16,32,128]{3,2,1,0:T(8,128)}, u32[]{:S(2)}) copy-start(f32[1,16,32,128]{3,2,1,0:T(8,128)} %refs_4_.1) | copy-start | bytes 786436
  33.2 6.0 %collective-permute-start.6 = (f32[8,32,128]{2,1,0:T(8,128)S(1)}, f32[8,32,128]{2,1,0:T(8,128)S(1)}, u32[]{:S(2)}, u32[]{:S(2)}) collective-permute-start(f32[8,32,128]{2,1,0:T(8,128)S(1)} %get-tuple-element.10), channel_id=1, source_target_pairs={{0,1},{1,0},{2,3},{3,2},{4,5},{5,4},{6,7},{7,6},{8,9},{9,8},{10,11... | collective-permute-start | bytes 393224 | tf_op jit(solution)/shard_map/ppermute | solution.py:388
  39.2 9.0 %collective-permute-start.7 = (f32[8,32,128]{2,1,0:T(8,128)S(1)}, f32[8,32,128]{2,1,0:T(8,128)S(1)}, u32[]{:S(2)}, u32[]{:S(2)}) collective-permute-start(f32[8,32,128]{2,1,0:T(8,128)S(1)} %add.6), channel_id=1, source_target_pairs={{0,2},{1,3},{2,0},{3,1},{4,6},{5,7},{6,4},{7,5},{8,10},{9,11},{10,... | collective-permute-start | bytes 393224 | tf_op jit(solution)/shard_map/ppermute | solution.py:388
  48.3 5.0 %collective-permute-start.8 = (f32[8,32,128]{2,1,0:T(8,128)S(1)}, f32[8,32,128]{2,1,0:T(8,128)S(1)}, u32[]{:S(2)}, u32[]{:S(2)}) collective-permute-start(f32[8,32,128]{2,1,0:T(8,128)S(1)} %add.7), channel_id=1, source_target_pairs={{0,1},{1,0},{2,3},{3,2},{4,5},{5,4},{6,7},{7,6},{8,9},{9,8},{10,11... | collective-permute-start | bytes 393224 | tf_op jit(solution)/shard_map/ppermute | solution.py:388

commit v3 on v2

--- a/solution.py
+++ b/solution.py
@@ -223,8 +223,13 @@
 def kernel(masks, total, ints, currents, observed, *refs):
     parts = len(masks)
     sigma_parts, prior_parts = refs[:parts], refs[parts : 2 * parts]
-    potential_out, misfit_out, keep_out, send_out = refs[2 * parts : 2 * parts + 4]
+    potential_out, misfit_out, low_out, high_out = refs[2 * parts : 2 * parts + 4]
     scratch = list(refs[2 * parts + 4 :])
+    sigma_own, prior_own, staged, arrived, left = [scratch.pop(0) for _ in range(5)]
+    sigma_copy = pltpu.make_async_copy(sigma_parts[0], sigma_own, arrived.at[0])
+    prior_copy = pltpu.make_async_copy(prior_parts[0], prior_own, arrived.at[1])
+    sigma_copy.start()
+    prior_copy.start()
     forward = scratch.pop(0)
     local = prior_parts[0].shape[1]
     levels = []
@@ -234,8 +239,8 @@
         levels.append(Level(index, total >> index, *arrays, sigma))
     fine = levels[0]
     adjoint = fine.field
-    position, half = ints[0], ints[1]
-    receivers = ints.shape[0] - 4
+    position = ints[0]
+    receivers = ints.shape[0] - 3
     zero = jnp.zeros((SUB, LANES), jnp.float32)
 
     for level in levels:
@@ -244,7 +249,11 @@
                 ref[0, j] = zero
                 ref[level.planes + 1, j] = zero
 
-    for mask, sigma_part, prior_part in zip(masks, sigma_parts, prior_parts):
+    for mask, sigma_part, prior_part in reversed(list(zip(masks, sigma_parts, prior_parts))):
+        if mask == 0:
+            sigma_copy.wait()
+            prior_copy.wait()
+            sigma_part, prior_part = sigma_own, prior_own
         base = (position ^ mask) * local
 
         def place(plane, carry, base=base, sigma_part=sigma_part, prior_part=prior_part):
@@ -266,7 +275,7 @@
 
     lane = lax.broadcasted_iota(jnp.int32, (1, LANES), 1)
     for which, sign in ((0, 2.0), (1, -2.0)):
-        x, j, s, z = cell_of(ints[2 + which])
+        x, j, s, z = cell_of(ints[1 + which])
         row = fine.right[x, j, pl.ds(s, 1), :]
         fine.right[x, j, pl.ds(s, 1), :] = row + jnp.where(lane == z, sign * currents[0], 0.0)
 
@@ -278,20 +287,29 @@
     half_sweep(fine, forward, 0)
     half_sweep(fine, forward, 1)
 
+    first = position * local
+
+    def deliver(plane, carry):
+        for j in range(4):
+            staged[0, plane, pl.ds(j, SUB, stride=4), :] = forward[first + plane + 1, j]
+        return carry
+
+    lax.fori_loop(0, local, deliver, 0, unroll=16)
+    potential_copy = pltpu.make_async_copy(staged, potential_out, left)
+    potential_copy.start()
+
     for which in range(2):
-        x, j, s, z = cell_of(ints[2 + which])
+        x, j, s, z = cell_of(ints[1 + which])
         fine.right[x, j, pl.ds(s, 1), :] = jnp.zeros((1, LANES), jnp.float32)
 
     def receive(k, carry):
-        x, j, s, z = cell_of(ints[4 + k])
-        value = jnp.where(lane == z, forward[x + 1, j, pl.ds(s, 1), :] - observed[k], 0.0)
+        x, j, s, z = cell_of(ints[3 + k])
+        value = jnp.where(lane == z, forward[x + 1, j, pl.ds(s, 1), :] - observed[0, k], 0.0)
         misfit_out[pl.ds(k, 1), :] = value
         fine.right[x, j, pl.ds(s, 1), :] = fine.right[x, j, pl.ds(s, 1), :] + 2.0 * value
         return carry
 
     lax.fori_loop(0, receivers, receive, 0, unroll=32)
-
-    first = position * local
 
     def window(margin):
         count = min(local + 2 * margin, fine.planes)
@@ -337,14 +355,9 @@
 
         lax.fori_loop(0, local // 2, plane_of, 0, unroll=8)
 
-    def deliver(plane, carry):
-        for j in range(4):
-            potential_out[0, plane, pl.ds(j, SUB, stride=4), :] = forward[first + plane + 1, j]
-        return carry
-
-    gradient(first + half * (local // 2), keep_out, 0)
-    gradient(first + (1 - half) * (local // 2), send_out, 0)
-    lax.fori_loop(0, local, deliver, 0, unroll=16)
+    gradient(first, low_out, 0)
+    gradient(first + local // 2, high_out, 0)
+    potential_copy.wait()
 
 
 def solve(sigma_parts, prior_parts, masks, ints, currents, observed):
@@ -356,18 +369,21 @@
     def planes(count, index):
         return pltpu.VMEM((count, ROWS[index], SUB, LANES), jnp.float32)
 
-    scratch = [planes(total + 2, 0)]
+    slab = (local, cells_y, cells_z)
+    scratch = [pltpu.VMEM(slab, jnp.float32), pltpu.VMEM((1, *slab), jnp.float32), pltpu.VMEM((1, *slab), jnp.float32)]
+    scratch += [pltpu.SemaphoreType.DMA((2,)), pltpu.SemaphoreType.DMA, planes(total + 2, 0)]
     for index in range(LEVELS):
         n = total >> index
         scratch += [planes(n + 2, index), planes(n, index), planes(n + 1, index)]
         scratch += [planes(n, index) for _ in range(4)]
         if index:
             scratch.append(planes(n + 2, index))
-    held = 4 * sum(s.shape[0] * s.shape[1] * SUB * LANES for s in scratch)
-    held += 4 * cells_y * cells_z * local * (2 * parts + 2) + 4 * LANES * receivers
+    held = 4 * sum(s.shape[0] * s.shape[1] * SUB * LANES for s in scratch[5:])
+    held += 4 * cells_y * cells_z * local * (2 * parts + 3) + 4 * LANES * receivers
     half = jax.ShapeDtypeStruct((local // 2, cells_y, cells_z), jnp.float32)
     smem = pl.BlockSpec(memory_space=pltpu.SMEM)
     vmem = pl.BlockSpec(memory_space=pltpu.VMEM)
+    anywhere = pl.BlockSpec(memory_space=pl.ANY)
     return pl.pallas_call(
         functools.partial(kernel, masks, total),
         out_shape=(
@@ -376,8 +392,8 @@
             half,
             half,
         ),
-        in_specs=[smem] * 3 + [vmem] * (2 * parts),
-        out_specs=[vmem] * 4,
+        in_specs=[smem] * 3 + ([anywhere] + [vmem] * (parts - 1)) * 2,
+        out_specs=[anywhere] + [vmem] * 3,
         scratch_shapes=scratch,
         compiler_params=pltpu.CompilerParams(vmem_limit_bytes=min(held + (6 << 20), 63 << 20)),
         name="both_cycles",
@@ -391,7 +407,6 @@
 def body(conductivity, prior_potential, electrodes, currents, receivers, observed):
     count = lax.axis_size("space")
     position = lax.axis_index("space")
-    source = lax.axis_index("src")
     sigma_parts, prior_parts, masks = [conductivity], [prior_potential], [0]
     bit = count // 2
     while bit:
@@ -399,22 +414,20 @@
         prior_parts += [exchanged(part, "space", bit) for part in prior_parts]
         masks += [mask ^ bit for mask in masks]
         bit //= 2
-    upper = source & 1
-    ints = jnp.concatenate([jnp.stack([position, upper]), electrodes[0], receivers])
-    potential, picked, keep, send = solve(
-        sigma_parts, prior_parts, tuple(masks), ints, currents, observed[0]
+    ints = jnp.concatenate([position[None], electrodes[0], receivers])
+    potential, picked, low, high = solve(
+        sigma_parts, prior_parts, tuple(masks), ints, currents, observed
     )
     misfit = jnp.sum(picked, axis=1)[None, :]
-    summed = keep + exchanged(send, "src", 1)
-    bit = 2
-    while bit < lax.axis_size("src"):
-        summed = summed + exchanged(summed, "src", bit)
-        bit *= 2
-    other = exchanged(summed, "src", 1)
-    gradient = jnp.concatenate(
-        [jnp.where(upper == 1, other, summed), jnp.where(upper == 1, summed, other)], 0
-    )
-    return potential, misfit, gradient
+    orders = [[1], [1]]
+    while orders[0][-1] < lax.axis_size("src") - 1:
+        step = 2 * orders[0][-1] + 1
+        orders = [orders[0] + [step], orders[1][:-1] + [step, orders[1][-1]]]
+    for step_low, step_high in zip(*orders):
+        from_low = exchanged(low, "src", step_low)
+        from_high = exchanged(high, "src", step_high)
+        low, high = low + from_low, high + from_high
+    return potential, misfit, jnp.concatenate([low, high], 0)
 
 
 def solution(mesh):

time: 54.3 us -> 51.6 us (0.950)
  waiting for transfers between devices: 25.6 us -> 17.5 us
  starting transfers between devices: 9.03 us -> 15.1 us
  Pallas kernels: 13.5 us -> 12.9 us
    ppermute x9 -> x10, waiting for transfers between devices: 25.6 us -> 17.5 us  [exchanged(): lax.ppermute(value, axis, [(i, i ^ mask) for i in range(lax.axis_size(axi...]
    ppermute x9 -> x10, starting transfers between devices: 9.03 us -> 15.1 us  [exchanged(): lax.ppermute(value, axis, [(i, i ^ mask) for i in range(lax.axis_size(axi...]
    pallas_call x1, Pallas kernels: 13.5 us -> 12.9 us  [solve(): pl.pallas_call(functools.partial(kernel, masks, total), out_shape=(jax.Sh...]
  transfers between devices with their start and end apart: 9 -> 10, of which waited for: 6 -> 6; matrix products, arithmetic and copies ran while one was open for 1% -> 2% of each run, Pallas kernels for 0% -> 0%
where the time goes in v3:
time: 51.6 us; the launch traced here: 51.4 us
  waiting for transfers between devices  17.5 us (34%)
  starting transfers between devices  15.1 us (29%)
  Pallas kernels  12.9 us (25%)
  local copies, waits for them, and re-layouts  3.05 us (6%)
  other arithmetic  1.55 us (3%)
  between operations  1.34 us (3%)
    ppermute x10, waiting for transfers between devices, exchanged(): lax.ppermute(value, axis, [(i, i ^ mask) for i in range(lax.axis_size(axi...  17.5 us
    ppermute x10, starting transfers between devices, exchanged(): lax.ppermute(value, axis, [(i, i ^ mask) for i in range(lax.axis_size(axi...  15.1 us
    pallas_call x1, Pallas kernels, solve(): pl.pallas_call(functools.partial(kernel, masks, total), out_shape=(jax.Sh...  12.9 us
    unnamed x10, local copies, waits for them, and re-layouts  3.05 us
  transfers between devices with their start and end apart: 10, of which 6 were waited for; matrix products, arithmetic and copies ran while one was open for 2% of the time, Pallas kernels for 0%

profile of v3, /device:TPU:0, one launch (start us, length us, event | category | flops | bytes accessed | tf_op | source)
XLA Modules:
  0.0 51.4 jit_solution(8820821816606254723)
XLA Ops:
  0.6 3.0 %collective-permute-start = (f32[16,32,128]{2,1,0:T(8,128)}, f32[16,32,128]{2,1,0:T(8,128)S(1)}, u32[]{:S(2)}, u32[]{:S(2)}) collective-permute-start(f32[16,32,128]{2,1,0:T(8,128)} %refs_0_.1), channel_id=1, source_target_pairs={{0,8},{4,12},{8,0},{12,4},{1,9},{5,13},{9,1},{13,5},{2,10},{6,14},... | collective-permute-start | bytes 786440 | tf_op jit(solution)/shard_map/ppermute | solution.py:404
  3.6 0.1 collective-permute-start.3
  3.7 0.0 collective-permute-start.1
  3.7 0.5 collective-permute-start.4
  4.2 6.8 %collective-permute-done.refs_1_ = f32[16,32,128]{2,1,0:T(8,128)S(1)} collective-permute-done((f32[16,32,128]{2,1,0:T(8,128)}, f32[16,32,128]{2,1,0:T(8,128)S(1)}, u32[]{:S(2)}, u32[]{:S(2)}) %collective-permute-start) | collective-permute-done | bytes 262176 | tf_op jit(solution)/shard_map/ppermute | solution.py:404
  11.0 0.0 collective-permute-start.2
  11.0 4.8 %collective-permute-done.3.refs_5_ = f32[1,16,32,128]{3,2,1,0:T(8,128)S(1)} collective-permute-done((f32[1,16,32,128]{3,2,1,0:T(8,128)}, f32[1,16,32,128]{3,2,1,0:T(8,128)S(1)}, u32[]{:S(2)}, u32[]{:S(2)}) %collective-permute-start.3) | collective-permute-done | bytes 262176 | tf_op jit(solution)/shard_map/ppermute | solution.py:404
  15.8 0.0 collective-permute-start.5
  16.4 0.0 copy-start.3
  16.4 0.0 copy-start.4
  16.4 0.7 %copy-done.3 = s32[256]{0:T(256)S(1)} copy-done((s32[256]{0:T(256)S(1)}, s32[256]{0:T(256)}, u32[]{:S(2)}) %copy-start.3) | copy-done | bytes 1048
  17.1 0.0 copy-done.4
  17.1 0.0 copy-start.2
  17.1 0.1 pad_add_fusion.ints
  17.2 0.0 collective-permute-done.1.refs_2_
  17.2 0.0 collective-permute-done.4.refs_6_
  17.2 0.0 collective-permute-done.2.refs_3_
  17.2 0.1 collective-permute-done.5.refs_7_
  17.3 0.5 copy-done.2
  17.8 0.9 %copy-done = f32[16,32,128]{2,1,0:T(8,128)S(1)} copy-done((f32[16,32,128]{2,1,0:T(8,128)S(1)}, f32[16,32,128]{2,1,0:T(8,128)}, u32[]{:S(2)}) %copy-start) | copy-done | bytes 262168
  18.7 0.9 %copy-done.1 = f32[1,16,32,128]{3,2,1,0:T(8,128)S(1)} copy-done((f32[1,16,32,128]{3,2,1,0:T(8,128)S(1)}, f32[1,16,32,128]{3,2,1,0:T(8,128)}, u32[]{:S(2)}) %copy-start.1) | copy-done | bytes 262168
  19.7 12.9 %both_cycles.1 = (f32[1,16,32,128]{3,2,1,0:T(8,128)}, f32[256,128]{1,0:T(8,128)S(1)}, f32[8,32,128]{2,1,0:T(8,128)S(1)}, f32[8,32,128]{2,1,0:T(8,128)S(1)}) custom-call(s32[259]{0:T(512)S(1)} %pad_add_fusion.ints, f32[1]{0:T(128)S(6)} %copy.9.currents, f32[1,256]{1,0:T(1,128)S(1)} %copy-done.2, f32[16,32,128]{2,1,0:T(8,128)S(1)} %copy-done, ...), custom_call_target="tpu_custom_call" | custom-call | tf_op jit(solution)/shard_map/both_cycles/pallas_call | solution.py:387
  32.6 1.9 %collective-permute-start.6 = (f32[8,32,128]{2,1,0:T(8,128)S(1)}, f32[8,32,128]{2,1,0:T(8,128)S(1)}, u32[]{:S(2)}, u32[]{:S(2)}) collective-permute-start(f32[8,32,128]{2,1,0:T(8,128)S(1)} %get-tuple-element.9), channel_id=1, source_target_pairs={{0,1},{1,0},{2,3},{3,2},{4,5},{5,4},{6,7},{7,6},{8,9},{9,8},{10,11... | collective-permute-start | bytes 393224 | tf_op jit(solution)/shard_map/ppermute | solution.py:404
  34.5 2.5 %collective-permute-start.8 = (f32[8,32,128]{2,1,0:T(8,128)S(1)}, f32[8,32,128]{2,1,0:T(8,128)S(1)}, u32[]{:S(2)}, u32[]{:S(2)}) collective-permute-start(f32[8,32,128]{2,1,0:T(8,128)S(1)} %get-tuple-element.10), channel_id=1, source_target_pairs={{0,3},{1,2},{2,1},{3,0},{4,7},{5,6},{6,5},{7,4},{8,11},{9,10},{10,... | collective-permute-start | bytes 393224 | tf_op jit(solution)/shard_map/ppermute | solution.py:404
  37.0 1.7 %collective-permute-done.6 = f32[8,32,128]{2,1,0:T(8,128)S(1)} collective-permute-done((f32[8,32,128]{2,1,0:T(8,128)S(1)}, f32[8,32,128]{2,1,0:T(8,128)S(1)}, u32[]{:S(2)}, u32[]{:S(2)}) %collective-permute-start.6) | collective-permute-done | bytes 131104 | tf_op jit(solution)/shard_map/ppermute | solution.py:404
  38.7 6.6 %collective-permute-start.7 = (f32[8,32,128]{2,1,0:T(8,128)S(1)}, f32[8,32,128]{2,1,0:T(8,128)S(1)}, u32[]{:S(2)}, u32[]{:S(2)}) collective-permute-start(f32[8,32,128]{2,1,0:T(8,128)S(1)} %add.12), channel_id=1, source_target_pairs={{0,3},{1,2},{2,1},{3,0},{4,7},{5,6},{6,5},{7,4},{8,11},{9,10},{10,... | collective-permute-start | bytes 393224 | tf_op jit(solution)/shard_map/ppermute | solution.py:404
  45.3 0.0 collective-permute-done.8
  45.4 0.5 collective-permute-start.9
  45.8 0.7 %reduce_sum.9 = f32[256]{0:T(256)} reduce(f32[256,128]{1,0:T(8,128)S(1)} %get-tuple-element.8, f32[]{:T(128)} %constant.6.clone.1), dimensions={1}, to_apply=%region_0.0 | reduce | flops 32512 | bytes 132100 | tf_op jit(solution)/shard_map/reduce_sum | solution.py:421
  46.5 3.0 %collective-permute-done.7 = f32[8,32,128]{2,1,0:T(8,128)S(1)} collective-permute-done((f32[8,32,128]{2,1,0:T(8,128)S(1)}, f32[8,32,128]{2,1,0:T(8,128)S(1)}, u32[]{:S(2)}, u32[]{:S(2)}) %collective-permute-start.7) | collective-permute-done | bytes 131104 | tf_op jit(solution)/shard_map/ppermute | solution.py:404
  49.5 1.1 %collective-permute-done.9 = f32[8,32,128]{2,1,0:T(8,128)S(1)} collective-permute-done((f32[8,32,128]{2,1,0:T(8,128)S(1)}, f32[8,32,128]{2,1,0:T(8,128)S(1)}, u32[]{:S(2)}, u32[]{:S(2)}) %collective-permute-start.9) | collective-permute-done | bytes 131104 | tf_op jit(solution)/shard_map/ppermute | solution.py:404
  50.7 0.7 %pad_maximum_fusion = f32[16,32,128]{2,1,0:T(8,128)} fusion(f32[8,32,128]{2,1,0:T(8,128)S(1)} %add.15, f32[8,32,128]{2,1,0:T(8,128)S(1)} %add.13), kind=kLoop, calls=%fused_computation | loop fusion | flops 65536 | bytes 524288 | tf_op jit(solution)/shard_map/concatenate | solution.py:430
  (6 shorter events, 0.1 us)
Async XLA Ops:
  0.6 10.4 %collective-permute-start = (f32[16,32,128]{2,1,0:T(8,128)}, f32[16,32,128]{2,1,0:T(8,128)S(1)}, u32[]{:S(2)}, u32[]{:S(2)}) collective-permute-start(f32[16,32,128]{2,1,0:T(8,128)} %refs_0_.1), channel_id=1, source_target_pairs={{0,8},{4,12},{8,0},{12,4},{1,9},{5,13},{9,1},{13,5},{2,10},{6,14},... | collective-permute-start | bytes 786440 | tf_op jit(solution)/shard_map/ppermute | solution.py:404
  3.6 12.1 %collective-permute-start.3 = (f32[1,16,32,128]{3,2,1,0:T(8,128)}, f32[1,16,32,128]{3,2,1,0:T(8,128)S(1)}, u32[]{:S(2)}, u32[]{:S(2)}) collective-permute-start(f32[1,16,32,128]{3,2,1,0:T(8,128)} %refs_4_.1), channel_id=1, source_target_pairs={{0,8},{4,12},{8,0},{12,4},{1,9},{5,13},{9,1},{13,5},{2,10},{6,14},... | collective-permute-start | bytes 786440 | tf_op jit(solution)/shard_map/ppermute | solution.py:404
  3.7 13.5 %collective-permute-start.1 = (f32[16,32,128]{2,1,0:T(8,128)}, f32[16,32,128]{2,1,0:T(8,128)S(1)}, u32[]{:S(2)}, u32[]{:S(2)}) collective-permute-start(f32[16,32,128]{2,1,0:T(8,128)} %refs_0_.1), channel_id=1, source_target_pairs={{0,4},{4,0},{8,12},{12,8},{1,5},{5,1},{9,13},{13,9},{2,6},{6,2},{1... | collective-permute-start | bytes 786440 | tf_op jit(solution)/shard_map/ppermute | solution.py:404
  3.7 13.5 %collective-permute-start.4 = (f32[1,16,32,128]{3,2,1,0:T(8,128)}, f32[1,16,32,128]{3,2,1,0:T(8,128)S(1)}, u32[]{:S(2)}, u32[]{:S(2)}) collective-permute-start(f32[1,16,32,128]{3,2,1,0:T(8,128)} %refs_4_.1), channel_id=1, source_target_pairs={{0,4},{4,0},{8,12},{12,8},{1,5},{5,1},{9,13},{13,9},{2,6},{6,2},{1... | collective-permute-start | bytes 786440 | tf_op jit(solution)/shard_map/ppermute | solution.py:404
  11.0 6.2 %collective-permute-start.2 = (f32[16,32,128]{2,1,0:T(8,128)S(1)}, f32[16,32,128]{2,1,0:T(8,128)S(1)}, u32[]{:S(2)}, u32[]{:S(2)}) collective-permute-start(f32[16,32,128]{2,1,0:T(8,128)S(1)} %collective-permute-done.refs_1_), channel_id=1, source_target_pairs={{0,4},{4,0},{8,12},{12,8},{1,5},{5,1},{9,13},{13,9},{2,6},{6,2},{1... | collective-permute-start | bytes 786440 | tf_op jit(solution)/shard_map/ppermute | solution.py:404
  15.8 1.5 %collective-permute-start.5 = (f32[1,16,32,128]{3,2,1,0:T(8,128)S(1)}, f32[1,16,32,128]{3,2,1,0:T(8,128)S(1)}, u32[]{:S(2)}, u32[]{:S(2)}) collective-permute-start(f32[1,16,32,128]{3,2,1,0:T(8,128)S(1)} %collective-permute-done.3.refs_5_), channel_id=1, source_target_pairs={{0,4},{4,0},{8,12},{12,8},{1,5},{5,1},{9,13},{13,9},{2,6},{6,2},{1... | collective-permute-start | bytes 786440 | tf_op jit(solution)/shard_map/ppermute | solution.py:404
  16.4 0.7 %copy-start.3 = (s32[256]{0:T(256)S(1)}, s32[256]{0:T(256)}, u32[]{:S(2)}) copy-start(s32[256]{0:T(256)} %param.10) | copy-start | bytes 3076
  16.4 0.7 %copy-start.4 = (s32[1,2]{1,0:T(1,128)S(1)}, s32[1,2]{1,0:T(1,128)}, u32[]{:S(2)}) copy-start(s32[1,2]{1,0:T(1,128)} %param.8) | copy-start | bytes 28
  17.1 0.7 %copy-start.2 = (f32[1,256]{1,0:T(1,128)S(1)}, f32[1,256]{1,0:T(1,128)}, u32[]{:S(2)}) copy-start(f32[1,256]{1,0:T(1,128)} %observed.1) | copy-start | bytes 3076
  17.8 0.9 %copy-start = (f32[16,32,128]{2,1,0:T(8,128)S(1)}, f32[16,32,128]{2,1,0:T(8,128)}, u32[]{:S(2)}) copy-start(f32[16,32,128]{2,1,0:T(8,128)} %refs_0_.1) | copy-start | bytes 786436
  18.7 0.9 %copy-start.1 = (f32[1,16,32,128]{3,2,1,0:T(8,128)S(1)}, f32[1,16,32,128]{3,2,1,0:T(8,128)}, u32[]{:S(2)}) copy-start(f32[1,16,32,128]{3,2,1,0:T(8,128)} %refs_4_.1) | copy-start | bytes 786436
  32.6 6.1 %collective-permute-start.6 = (f32[8,32,128]{2,1,0:T(8,128)S(1)}, f32[8,32,128]{2,1,0:T(8,128)S(1)}, u32[]{:S(2)}, u32[]{:S(2)}) collective-permute-start(f32[8,32,128]{2,1,0:T(8,128)S(1)} %get-tuple-element.9), channel_id=1, source_target_pairs={{0,1},{1,0},{2,3},{3,2},{4,5},{5,4},{6,7},{7,6},{8,9},{9,8},{10,11... | collective-permute-start | bytes 393224 | tf_op jit(solution)/shard_map/ppermute | solution.py:404
  34.5 10.8 %collective-permute-start.8 = (f32[8,32,128]{2,1,0:T(8,128)S(1)}, f32[8,32,128]{2,1,0:T(8,128)S(1)}, u32[]{:S(2)}, u32[]{:S(2)}) collective-permute-start(f32[8,32,128]{2,1,0:T(8,128)S(1)} %get-tuple-element.10), channel_id=1, source_target_pairs={{0,3},{1,2},{2,1},{3,0},{4,7},{5,6},{6,5},{7,4},{8,11},{9,10},{10,... | collective-permute-start | bytes 393224 | tf_op jit(solution)/shard_map/ppermute | solution.py:404
  38.7 10.8 %collective-permute-start.7 = (f32[8,32,128]{2,1,0:T(8,128)S(1)}, f32[8,32,128]{2,1,0:T(8,128)S(1)}, u32[]{:S(2)}, u32[]{:S(2)}) collective-permute-start(f32[8,32,128]{2,1,0:T(8,128)S(1)} %add.12), channel_id=1, source_target_pairs={{0,3},{1,2},{2,1},{3,0},{4,7},{5,6},{6,5},{7,4},{8,11},{9,10},{10,... | collective-permute-start | bytes 393224 | tf_op jit(solution)/shard_map/ppermute | solution.py:404
  45.4 5.3 %collective-permute-start.9 = (f32[8,32,128]{2,1,0:T(8,128)S(1)}, f32[8,32,128]{2,1,0:T(8,128)S(1)}, u32[]{:S(2)}, u32[]{:S(2)}) collective-permute-start(f32[8,32,128]{2,1,0:T(8,128)S(1)} %add.14), channel_id=1, source_target_pairs={{0,1},{1,0},{2,3},{3,2},{4,5},{5,4},{6,7},{7,6},{8,9},{9,8},{10,11... | collective-permute-start | bytes 393224 | tf_op jit(solution)/shard_map/ppermute | solution.py:404

commit v4 on v3

--- a/solution.py
+++ b/solution.py
@@ -1,4 +1,5 @@
 import functools
+import math
 
 import jax
 import jax.numpy as jnp
@@ -215,175 +216,327 @@
     half_sweep(level, level.field, 1)
 
 
+class SigmaRows:
+    def __init__(self, ref):
+        self.ref = ref
+
+    def __getitem__(self, at):
+        return self.ref[at[1] // 2, at[0], at[1] % 2]
+
+    def __setitem__(self, at, value):
+        self.ref[at[1] // 2, at[0], at[1] % 2] = value
+
+
+class Fine:
+    def __init__(self, level, field, right, edge_x, edge_in, edge_out, edge_up, edge_down, diagonal, inverse):
+        self.level, self.planes, self.unroll = level, level.planes, level.unroll
+        self.field, self.right = field, right
+        self.edge_x, self.edge_in, self.edge_out = edge_x, edge_in, edge_out
+        self.edge_up, self.edge_down = edge_up, edge_down
+        self.diagonal, self.inverse = diagonal, inverse
+
+    def first_row(self, plane, colour):
+        return self.level.even if (plane + colour) % 2 == 0 else self.level.odd
+
+    def rows(self, field, at, plane):
+        first = self.first_row(plane, 0)
+        red = [field[0, at, k] for k in range(2)]
+        black = [field[1, at, k] for k in range(2)]
+        return [
+            jnp.where(first, red[k], black[k]) if j == 0 else jnp.where(first, black[k], red[k])
+            for k in range(2)
+            for j in range(2)
+        ]
+
+
+def fine_setup(fine, sigma):
+    level = fine.level
+
+    def body(base, count):
+        for p in range(count):
+            mid = [sigma[base + p + 1, j] for j in range(4)]
+            over = [sigma[base + p + 2, j] for j in range(4)]
+            under = [sigma[base + p, j] for j in range(4)]
+            edge_x = [m + o for m, o in zip(mid, over)]
+            y_above = mid[1:] + [jnp.where(level.last_y, 0.0, level.y_up(mid[0]))]
+            y_below = [jnp.where(level.first_y, 0.0, level.y_down(mid[3]))] + mid[:3]
+            z_above = [jnp.where(level.last_z, 0.0, level.z_up(m)) for m in mid]
+            z_below = [jnp.where(level.first_z, 0.0, level.z_down(m)) for m in mid]
+            edge_y = [m + a for m, a in zip(mid, y_above)]
+            edge_y[3] = jnp.where(level.last_y, 0.0, edge_y[3])
+            edge_y_below = [level.y_down(edge_y[3])] + edge_y[:3]
+            edge_up = [jnp.where(level.last_z, 0.0, m + a) for m, a in zip(mid, z_above)]
+            edge_down = [jnp.where(level.first_z, 0.0, m + b) for m, b in zip(mid, z_below)]
+            diagonal = [
+                edge_x[j] + (mid[j] + under[j]) + (4.0 * mid[j] + ((y_above[j] + y_below[j]) + (z_above[j] + z_below[j])))
+                for j in range(4)
+            ]
+            for k in range(2):
+                fine.edge_in[base + p, k] = edge_y[2 * k]
+                for colour in range(2):
+                    first = fine.first_row(p, colour)
+
+                    def packed(rows, k=k, first=first):
+                        return jnp.where(first, rows[2 * k], rows[2 * k + 1])
+
+                    total = packed(diagonal)
+                    fine.edge_x[colour, base + p + 1, k] = packed(edge_x)
+                    fine.edge_out[colour, base + p, k] = jnp.where(first, edge_y_below[2 * k], edge_y[2 * k + 1])
+                    fine.edge_up[colour, base + p, k] = packed(edge_up)
+                    fine.edge_down[colour, base + p, k] = packed(edge_down)
+                    fine.diagonal[colour, base + p, k] = total
+                    fine.inverse[colour, base + p, k] = 1.0 / total
+
+    for colour in range(2):
+        for k in range(2):
+            fine.edge_x[colour, 0, k] = jnp.zeros((SUB, LANES), jnp.float32)
+    blocks(level, body)
+
+
+def fine_gathered(fine, field, colour, base, count):
+    level = fine.level
+    other = [[field[1 - colour, base + p, k] for k in range(2)] for p in range(count + 2)]
+    sums = []
+    for p in range(count):
+        mid = other[p + 1]
+        first = fine.first_row(p, colour)
+        y_out = [
+            jnp.where(first, level.y_down(mid[1]), mid[1]),
+            jnp.where(first, mid[0], level.y_up(mid[0])),
+        ]
+        for k in range(2):
+            total = fine.right[colour, base + p, k] + fine.edge_x[colour, base + p + 1, k] * other[p + 2][k]
+            total = total + fine.edge_x[1 - colour, base + p, k] * other[p][k]
+            total = total + fine.edge_in[base + p, k] * mid[k]
+            total = total + fine.edge_out[colour, base + p, k] * y_out[k]
+            z_sum = fine.edge_up[colour, base + p, k] * level.z_up(mid[k])
+            z_sum = z_sum + fine.edge_down[colour, base + p, k] * level.z_down(mid[k])
+            sums.append(total + z_sum)
+    return sums
+
+
+def fine_half_sweep(fine, field, colour, window=None):
+    def body(base, count):
+        for at, total in enumerate(fine_gathered(fine, field, colour, base, count)):
+            p, k = at // 2, at % 2
+            field[colour, base + p + 1, k] = total * fine.inverse[colour, base + p, k]
+
+    blocks(fine.level, body, window)
+
+
+def fine_red_from_zero(fine, field):
+    def body(base, count):
+        for p in range(count):
+            for k in range(2):
+                field[0, base + p + 1, k] = fine.right[0, base + p, k] * fine.inverse[0, base + p, k]
+
+    blocks(fine.level, body)
+
+
+def fine_restrict_residual(fine, field, coarse):
+    level = fine.level
+
+    def body(base, count):
+        left = [0.0] * (2 * count)
+        for colour in range(2):
+            for at, total in enumerate(fine_gathered(fine, field, colour, base, count)):
+                p, k = at // 2, at % 2
+                left[at] += total - fine.diagonal[colour, base + p, k] * field[colour, base + p + 1, k]
+        for p in range(0, count, 2):
+            for k in range(2):
+                value = left[2 * p + k] + left[2 * p + 2 + k]
+                value = value + jnp.where(level.z_even, level.z_up(value), level.z_down(value))
+                coarse.right[base // 2 + p // 2, k] = 0.5 * value
+
+    blocks(level, body)
+
+
+def fine_correct(fine, field, coarse, window=None):
+    def body(base, count):
+        for p in range(count):
+            for k in range(2):
+                e = coarse.field[base // 2 + p // 2 + 1, k]
+                field[1, base + p + 1, k] = field[1, base + p + 1, k] + e
+
+    blocks(fine.level, body, window)
+
+
 def cell_of(flat):
-    y = (flat >> 7) & 31
-    return flat >> 12, y & 3, y >> 2, flat & 127
-
-
-def kernel(masks, total, ints, currents, observed, *refs):
+    x, y, z = flat >> 12, (flat >> 7) & 31, flat & 127
+    return (x + y + z) & 1, x, (y >> 1) & 1, y >> 2, z
+
+
+def kernel(masks, total, ints, floats, *refs):
     parts = len(masks)
     sigma_parts, prior_parts = refs[:parts], refs[parts : 2 * parts]
     potential_out, misfit_out, low_out, high_out = refs[2 * parts : 2 * parts + 4]
     scratch = list(refs[2 * parts + 4 :])
-    sigma_own, prior_own, staged, arrived, left = [scratch.pop(0) for _ in range(5)]
-    sigma_copy = pltpu.make_async_copy(sigma_parts[0], sigma_own, arrived.at[0])
-    prior_copy = pltpu.make_async_copy(prior_parts[0], prior_own, arrived.at[1])
-    sigma_copy.start()
-    prior_copy.start()
-    forward = scratch.pop(0)
-    local = prior_parts[0].shape[1]
-    levels = []
-    for index in range(LEVELS):
-        arrays = [scratch.pop(0) for _ in range(7)]
-        sigma = scratch.pop(0) if index else arrays[0]
-        levels.append(Level(index, total >> index, *arrays, sigma))
-    fine = levels[0]
+    staged, left, forward = [scratch.pop(0) for _ in range(3)]
+    local = prior_parts[0].shape[0]
+    fine = Fine(Level(0, total, *[None] * 8), *[scratch.pop(0) for _ in range(9)])
     adjoint = fine.field
+    sigma = SigmaRows(adjoint)
+    grid = fine.level
+    grid.sigma = sigma
+    levels = [grid] + [Level(index, total >> index, *[scratch.pop(0) for _ in range(8)]) for index in range(1, LEVELS)]
     position = ints[0]
     receivers = ints.shape[0] - 3
     zero = jnp.zeros((SUB, LANES), jnp.float32)
 
-    for level in levels:
-        for ref in [level.field] + ([level.sigma] if level.index else [forward]):
+    def clear_ends(field):
+        for colour in range(2):
+            for k in range(2):
+                field[colour, 0, k] = zero
+                field[colour, total + 1, k] = zero
+
+    for level in levels[1:]:
+        for ref in (level.field, level.sigma):
             for j in range(level.rows):
                 ref[0, j] = zero
                 ref[level.planes + 1, j] = zero
-
-    for mask, sigma_part, prior_part in reversed(list(zip(masks, sigma_parts, prior_parts))):
-        if mask == 0:
-            sigma_copy.wait()
-            prior_copy.wait()
-            sigma_part, prior_part = sigma_own, prior_own
+    clear_ends(forward)
+    clear_ends(adjoint)
+
+    for mask, sigma_part, prior_part in zip(masks, sigma_parts, prior_parts):
         base = (position ^ mask) * local
-
-        def place(plane, carry, base=base, sigma_part=sigma_part, prior_part=prior_part):
-            for j in range(ROWS[0]):
-                adjoint[base + plane + 1, j] = sigma_part[plane, pl.ds(j, SUB, stride=4), :]
-                forward[base + plane + 1, j] = prior_part[0, plane, pl.ds(j, SUB, stride=4), :]
-                fine.right[base + plane, j] = zero
-            return carry
-
-        lax.fori_loop(0, local, place, 0, unroll=16)
-
-    setup(fine)
+        for plane in range(local):
+            for j in range(4):
+                sigma[base + plane + 1, j] = sigma_part[plane, pl.ds(j, SUB, stride=4), :]
+            for k in range(2):
+                forward[1, base + plane + 1, k] = prior_part[plane, k]
+                for colour in range(2):
+                    fine.right[colour, base + plane, k] = zero
+
+    fine_setup(fine, sigma)
     for index in range(LEVELS - 1):
         restrict_sigma(levels[index], levels[index + 1])
         setup(levels[index + 1])
-    for j in range(ROWS[0]):
-        adjoint[0, j] = zero
-        adjoint[fine.planes + 1, j] = zero
+    clear_ends(adjoint)
 
     lane = lax.broadcasted_iota(jnp.int32, (1, LANES), 1)
     for which, sign in ((0, 2.0), (1, -2.0)):
-        x, j, s, z = cell_of(ints[1 + which])
-        row = fine.right[x, j, pl.ds(s, 1), :]
-        fine.right[x, j, pl.ds(s, 1), :] = row + jnp.where(lane == z, sign * currents[0], 0.0)
-
-    half_sweep(fine, forward, 0)
-    half_sweep(fine, forward, 1)
-    restrict_residual(fine, forward, levels[1])
+        colour, x, k, s, z = cell_of(ints[1 + which])
+        row = fine.right[colour, x, k, pl.ds(s, 1), :]
+        fine.right[colour, x, k, pl.ds(s, 1), :] = row + jnp.where(lane == z, sign * floats[0], 0.0)
+
+    fine_half_sweep(fine, forward, 0)
+    fine_half_sweep(fine, forward, 1)
+    fine_restrict_residual(fine, forward, levels[1])
     coarse_solve(levels, 1)
-    correct(fine, forward, levels[1])
-    half_sweep(fine, forward, 0)
-    half_sweep(fine, forward, 1)
+    fine_correct(fine, forward, levels[1])
+    fine_half_sweep(fine, forward, 0)
+    fine_half_sweep(fine, forward, 1)
 
     first = position * local
-
-    def deliver(plane, carry):
-        for j in range(4):
-            staged[0, plane, pl.ds(j, SUB, stride=4), :] = forward[first + plane + 1, j]
-        return carry
-
-    lax.fori_loop(0, local, deliver, 0, unroll=16)
+    for plane in range(local):
+        for j, row in enumerate(fine.rows(forward, first + plane + 1, plane)):
+            staged[0, plane, pl.ds(j, SUB, stride=4), :] = row
     potential_copy = pltpu.make_async_copy(staged, potential_out, left)
     potential_copy.start()
 
     for which in range(2):
-        x, j, s, z = cell_of(ints[1 + which])
-        fine.right[x, j, pl.ds(s, 1), :] = jnp.zeros((1, LANES), jnp.float32)
-
-    def receive(k, carry):
-        x, j, s, z = cell_of(ints[3 + k])
-        value = jnp.where(lane == z, forward[x + 1, j, pl.ds(s, 1), :] - observed[0, k], 0.0)
-        misfit_out[pl.ds(k, 1), :] = value
-        fine.right[x, j, pl.ds(s, 1), :] = fine.right[x, j, pl.ds(s, 1), :] + 2.0 * value
+        colour, x, k, s, z = cell_of(ints[1 + which])
+        fine.right[colour, x, k, pl.ds(s, 1), :] = jnp.zeros((1, LANES), jnp.float32)
+
+    def receive(i, carry):
+        colour, x, k, s, z = cell_of(ints[3 + i])
+        value = jnp.where(lane == z, forward[colour, x + 1, k, pl.ds(s, 1), :] - floats[1 + i], 0.0)
+        misfit_out[pl.ds(i, 1), :] = value
+        fine.right[colour, x, k, pl.ds(s, 1), :] = fine.right[colour, x, k, pl.ds(s, 1), :] + 2.0 * value
         return carry
 
     lax.fori_loop(0, receivers, receive, 0, unroll=32)
 
     def window(margin):
-        count = min(local + 2 * margin, fine.planes)
-        return jnp.clip(first - margin, 0, fine.planes - count), count
-
-    red_from_zero(fine, adjoint)
-    half_sweep(fine, adjoint, 1)
-    restrict_residual(fine, adjoint, levels[1])
+        count = min(local + 2 * margin, total)
+        return jnp.clip(first - margin, 0, total - count), count
+
+    fine_red_from_zero(fine, adjoint)
+    fine_half_sweep(fine, adjoint, 1)
+    fine_restrict_residual(fine, adjoint, levels[1])
     coarse_solve(levels, 1)
-    correct(fine, adjoint, levels[1], window(4))
-    half_sweep(fine, adjoint, 0, window(2))
-    half_sweep(fine, adjoint, 1, window(2))
-
-    def gradient(base, out, out_base):
-        def plane_of(plane, carry):
-            at = base + plane + 1
-            p = [forward[at, j] for j in range(4)]
-            a = [adjoint[at, j] for j in range(4)]
+    fine_correct(fine, adjoint, levels[1], window(4))
+    fine_half_sweep(fine, adjoint, 0, window(2))
+    fine_half_sweep(fine, adjoint, 1, window(2))
+
+    def gradient(base, out):
+        ahead = [[fine.rows(field, base + p, p + 1) for field in (forward, adjoint)] for p in range(2)]
+        for plane in range(local // 2):
+            (under_p, under_a), (p, a) = ahead
+            over_p, over_a = [fine.rows(field, base + plane + 2, plane + 1) for field in (forward, adjoint)]
+            ahead = [(p, a), (over_p, over_a)]
             y_pairs = []
             for j in range(4):
                 if j < 3:
                     up_p, up_a = p[j + 1], a[j + 1]
                 else:
-                    up_p = jnp.where(fine.last_y, 0.0, fine.y_up(p[0]))
-                    up_a = jnp.where(fine.last_y, 0.0, fine.y_up(a[0]))
+                    up_p = jnp.where(grid.last_y, 0.0, grid.y_up(p[0]))
+                    up_a = jnp.where(grid.last_y, 0.0, grid.y_up(a[0]))
                 y_pairs.append((p[j] - up_p) * (a[j] - up_a))
             for j in range(4):
                 own = p[j] * a[j]
-                value = (p[j] - forward[at - 1, j]) * (a[j] - adjoint[at - 1, j])
-                value = value + (p[j] - forward[at + 1, j]) * (a[j] - adjoint[at + 1, j])
+                value = (p[j] - under_p[j]) * (a[j] - under_a[j])
+                value = value + (p[j] - over_p[j]) * (a[j] - over_a[j])
                 if j > 0:
                     y_below = y_pairs[j - 1]
                 else:
-                    y_below = jnp.where(fine.first_y, own, fine.y_down(y_pairs[3]))
+                    y_below = jnp.where(grid.first_y, own, grid.y_down(y_pairs[3]))
                 value = value + (y_pairs[j] + y_below)
-                up_p = jnp.where(fine.last_z, 0.0, fine.z_up(p[j]))
-                up_a = jnp.where(fine.last_z, 0.0, fine.z_up(a[j]))
+                up_p = jnp.where(grid.last_z, 0.0, grid.z_up(p[j]))
+                up_a = jnp.where(grid.last_z, 0.0, grid.z_up(a[j]))
                 z_pair = (p[j] - up_p) * (a[j] - up_a)
-                z_below = jnp.where(fine.first_z, own, fine.z_down(z_pair))
+                z_below = jnp.where(grid.first_z, own, grid.z_down(z_pair))
                 value = value + (z_pair + z_below)
-                out[out_base + plane, pl.ds(j, SUB, stride=4), :] = -0.5 * value
-            return carry
-
-        lax.fori_loop(0, local // 2, plane_of, 0, unroll=8)
-
-    gradient(first, low_out, 0)
-    gradient(first + local // 2, high_out, 0)
+                out[plane, pl.ds(j, SUB, stride=4), :] = -0.5 * value
+
+    gradient(first, low_out)
+    gradient(first + local // 2, high_out)
     potential_copy.wait()
 
 
-def solve(sigma_parts, prior_parts, masks, ints, currents, observed):
+def black_kernel(prior, out):
+    fine = Fine(Level(0, prior.shape[1], *[None] * 8), *[None] * 9)
+    for plane in range(prior.shape[1]):
+        first = fine.first_row(plane, 1)
+        rows = [prior[0, plane, pl.ds(j, SUB, stride=4), :] for j in range(4)]
+        for k in range(2):
+            out[plane, k] = jnp.where(first, rows[2 * k], rows[2 * k + 1])
+
+
+def black_cells(prior):
+    return pl.pallas_call(
+        black_kernel,
+        out_shape=jax.ShapeDtypeStruct((prior.shape[1], 2, SUB, LANES), jnp.float32),
+        name="black_cells",
+    )(prior)
+
+
+def solve(sigma_parts, prior_parts, masks, ints, floats):
     local, cells_y, cells_z = sigma_parts[0].shape
     parts = len(masks)
     total = local * parts
-    receivers = observed.shape[-1]
+    receivers = floats.shape[0] - 1
 
     def planes(count, index):
         return pltpu.VMEM((count, ROWS[index], SUB, LANES), jnp.float32)
 
+    def packed(count):
+        return pltpu.VMEM((2, count, 2, SUB, LANES), jnp.float32)
+
     slab = (local, cells_y, cells_z)
-    scratch = [pltpu.VMEM(slab, jnp.float32), pltpu.VMEM((1, *slab), jnp.float32), pltpu.VMEM((1, *slab), jnp.float32)]
-    scratch += [pltpu.SemaphoreType.DMA((2,)), pltpu.SemaphoreType.DMA, planes(total + 2, 0)]
-    for index in range(LEVELS):
+    scratch = [pltpu.VMEM((1, *slab), jnp.float32), pltpu.SemaphoreType.DMA, packed(total + 2)]
+    scratch += [packed(total + 2), packed(total), packed(total + 1)]
+    scratch += [pltpu.VMEM((total, 2, SUB, LANES), jnp.float32)] + [packed(total) for _ in range(5)]
+    for index in range(1, LEVELS):
         n = total >> index
         scratch += [planes(n + 2, index), planes(n, index), planes(n + 1, index)]
-        scratch += [planes(n, index) for _ in range(4)]
-        if index:
-            scratch.append(planes(n + 2, index))
-    held = 4 * sum(s.shape[0] * s.shape[1] * SUB * LANES for s in scratch[5:])
+        scratch += [planes(n, index) for _ in range(4)] + [planes(n + 2, index)]
+    held = 4 * sum(math.prod(s.shape) for s in scratch[2:])
     held += 4 * cells_y * cells_z * local * (2 * parts + 3) + 4 * LANES * receivers
     half = jax.ShapeDtypeStruct((local // 2, cells_y, cells_z), jnp.float32)
     smem = pl.BlockSpec(memory_space=pltpu.SMEM)
     vmem = pl.BlockSpec(memory_space=pltpu.VMEM)
-    anywhere = pl.BlockSpec(memory_space=pl.ANY)
+    hbm = pl.BlockSpec(memory_space=pl.ANY)
     return pl.pallas_call(
         functools.partial(kernel, masks, total),
         out_shape=(
@@ -392,12 +545,12 @@
             half,
             half,
         ),
-        in_specs=[smem] * 3 + ([anywhere] + [vmem] * (parts - 1)) * 2,
-        out_specs=[anywhere] + [vmem] * 3,
+        in_specs=[smem] * 2 + [vmem] * (2 * parts),
+        out_specs=[hbm] + [vmem] * 3,
         scratch_shapes=scratch,
         compiler_params=pltpu.CompilerParams(vmem_limit_bytes=min(held + (6 << 20), 63 << 20)),
         name="both_cycles",
-    )(ints, currents, observed, *sigma_parts, *prior_parts)
+    )(ints, floats, *sigma_parts, *prior_parts)
 
 
 def exchanged(value, axis, mask):
@@ -407,16 +560,28 @@
 def body(conductivity, prior_potential, electrodes, currents, receivers, observed):
     count = lax.axis_size("space")
     position = lax.axis_index("space")
-    sigma_parts, prior_parts, masks = [conductivity], [prior_potential], [0]
+    black = black_cells(prior_potential)
+    sigma_parts, prior_parts, masks = [conductivity], [black], [0]
     bit = count // 2
     while bit:
         sigma_parts += [exchanged(part, "space", bit) for part in sigma_parts]
-        prior_parts += [exchanged(part, "space", bit) for part in prior_parts]
+        if bit > 1:
+            prior_parts += [exchanged(part, "space", bit) for part in prior_parts]
         masks += [mask ^ bit for mask in masks]
         bit //= 2
     ints = jnp.concatenate([position[None], electrodes[0], receivers])
+    floats = jnp.concatenate([currents, observed[0]])
+    pair = masks.index(1)
+    sigma_back = exchanged(sigma_parts[pair], "space", 1)
+    prior_pair = exchanged(black, "space", 1)
+    prior_back = exchanged(prior_pair, "space", 1)
+    *far, sigma_back, prior_pair, prior_back, ints, floats = lax.optimization_barrier(
+        (*prior_parts[1:], sigma_back, prior_pair, prior_back, ints, floats)
+    )
+    sigma_parts[0] = sigma_back
+    prior_parts = [prior_back, *far, prior_pair] + [exchanged(part, "space", 1) for part in far]
     potential, picked, low, high = solve(
-        sigma_parts, prior_parts, tuple(masks), ints, currents, observed
+        sigma_parts, prior_parts, tuple(masks), ints, floats
     )
     misfit = jnp.sum(picked, axis=1)[None, :]
     orders = [[1], [1]]

time: 51.6 us -> 45.7 us (0.89)
  waiting for transfers between devices: 17.5 us -> 12.7 us
  local copies, waits for them, and re-layouts: 3.05 us -> 0.69 us
  Pallas kernels: 12.9 us -> 13.6 us
    ppermute x10 -> x12, waiting for transfers between devices: 17.5 us -> 12.7 us  [exchanged(): lax.ppermute(value, axis, [(i, i ^ mask) for i in range(lax.axis_size(axi...]
    unnamed x10 -> x6, local copies, waits for them, and re-layouts: 3.05 us -> 0.69 us
    pallas_call x0 -> x1, Pallas kernels: none -> 1.62 us  [black_cells(): pl.pallas_call(black_kernel, out_shape=jax.ShapeDtypeStruct((prior.shape[...]
    pallas_call x1, Pallas kernels: 12.9 us -> 12 us  [solve(): pl.pallas_call(functools.partial(kernel, masks, total), out_shape=(jax.Sh...]
    ppermute x10 -> x12, starting transfers between devices: 15.1 us -> 15.5 us  [exchanged(): lax.ppermute(value, axis, [(i, i ^ mask) for i in range(lax.axis_size(axi...]
  transfers between devices with their start and end apart: 10 -> 12, of which waited for: 6 -> 7; matrix products, arithmetic and copies ran while one was open for 2% -> 2% of each run, Pallas kernels for 0% -> 4%
where the time goes in v4:
time: 45.7 us; the launch traced here: 45.5 us
  starting transfers between devices  15.5 us (34%)
  Pallas kernels  13.6 us (30%)
  waiting for transfers between devices  12.7 us (28%)
  other arithmetic  1.62 us (4%)
  between operations  1.34 us (3%)
  local copies, waits for them, and re-layouts  0.69 us (2%)
    ppermute x12, starting transfers between devices, exchanged(): lax.ppermute(value, axis, [(i, i ^ mask) for i in range(lax.axis_size(axi...  15.5 us
    ppermute x12, waiting for transfers between devices, exchanged(): lax.ppermute(value, axis, [(i, i ^ mask) for i in range(lax.axis_size(axi...  12.7 us
    pallas_call x1, Pallas kernels, solve(): pl.pallas_call(functools.partial(kernel, masks, total), out_shape=(jax.Sh...  12 us
    pallas_call x1, Pallas kernels, black_cells(): pl.pallas_call(black_kernel, out_shape=jax.ShapeDtypeStruct((prior.shape[...  1.62 us
  transfers between devices with their start and end apart: 12, of which 7 were waited for; matrix products, arithmetic and copies ran while one was open for 2% of the time, Pallas kernels for 4%

profile of v4, /device:TPU:0, one launch (start us, length us, event | category | flops | bytes accessed | tf_op | source)
XLA Modules:
  0.0 45.5 jit_solution(15098396536658333530)
XLA Ops:
  0.6 0.5 %collective-permute-start.1 = (f32[16,32,128]{2,1,0:T(8,128)}, f32[16,32,128]{2,1,0:T(8,128)S(1)}, u32[]{:S(2)}, u32[]{:S(2)}) collective-permute-start(f32[16,32,128]{2,1,0:T(8,128)} %param.6), channel_id=1, source_target_pairs={{0,4},{4,0},{8,12},{12,8},{1,5},{5,1},{9,13},{13,9},{2,6},{6,2},{1... | collective-permute-start | bytes 786440 | tf_op jit(solution)/shard_map/ppermute | solution.py:557
  1.1 2.6 %collective-permute-start.5 = (f32[16,32,128]{2,1,0:T(8,128)}, f32[16,32,128]{2,1,0:T(8,128)S(1)}, u32[]{:S(2)}, u32[]{:S(2)}) collective-permute-start(f32[16,32,128]{2,1,0:T(8,128)} %param.6), channel_id=1, source_target_pairs={{0,8},{4,12},{8,0},{12,4},{1,9},{5,13},{9,1},{13,5},{2,10},{6,14},... | collective-permute-start | bytes 786440 | tf_op jit(solution)/shard_map/ppermute | solution.py:557
  3.7 1.6 %black_cells.1 = f32[16,2,8,128]{3,2,1,0:T(8,128)} custom-call(f32[1,16,32,128]{3,2,1,0:T(8,128)} %prior.1), custom_call_target="tpu_custom_call" | custom-call | tf_op jit(solution)/shard_map/black_cells/pallas_call | solution.py:507
  5.3 0.2 collective-permute-start.3
  5.5 0.0 collective-permute-done.1.refs_2_
  5.5 0.3 collective-permute-start.2
  5.8 0.0 collective-permute-start
  6.5 0.0 copy-start
  6.5 0.4 collective-permute-done.3.refs_6_
  6.9 0.2 collective-permute-start.4
  7.1 4.0 %collective-permute-done.5.refs_1_ = f32[16,32,128]{2,1,0:T(8,128)S(1)} collective-permute-done((f32[16,32,128]{2,1,0:T(8,128)}, f32[16,32,128]{2,1,0:T(8,128)S(1)}, u32[]{:S(2)}, u32[]{:S(2)}) %collective-permute-start.5) | collective-permute-done | bytes 262176 | tf_op jit(solution)/shard_map/ppermute | solution.py:557
  11.1 0.0 collective-permute-start.6
  11.1 0.1 pad_maximum_fusion.1.floats
  11.2 0.7 %copy-done.1 = s32[256]{0:T(256)S(1)} copy-done((s32[256]{0:T(256)S(1)}, s32[256]{0:T(256)}, u32[]{:S(2)}) %copy-start.1) | copy-done | bytes 1048
  11.8 0.1 pad_add_fusion.ints
  11.9 1.7 %collective-permute-done.refs_5_ = f32[16,2,8,128]{3,2,1,0:T(8,128)S(1)} collective-permute-done((f32[16,2,8,128]{3,2,1,0:T(8,128)}, f32[16,2,8,128]{3,2,1,0:T(8,128)S(1)}, u32[]{:S(2)}, u32[]{:S(2)}) %collective-permute-start) | collective-permute-done | bytes 131104 | tf_op jit(solution)/shard_map/ppermute | solution.py:557
  13.6 0.0 collective-permute-done.4.refs_4_
  13.6 0.0 collective-permute-done.2.refs_0_
  13.6 0.0 collective-permute-start.7
  13.6 0.0 collective-permute-done.6.refs_3_
  13.7 1.3 %collective-permute-done.7.refs_7_ = f32[16,2,8,128]{3,2,1,0:T(8,128)S(1)} collective-permute-done((f32[16,2,8,128]{3,2,1,0:T(8,128)S(1)}, f32[16,2,8,128]{3,2,1,0:T(8,128)S(1)}, u32[]{:S(2)}, u32[]{:S(2)}) %collective-permute-start.7) | collective-permute-done | bytes 131104 | tf_op jit(solution)/shard_map/ppermute | solution.py:557
  15.0 12.0 %both_cycles.1 = (f32[1,16,32,128]{3,2,1,0:T(8,128)}, f32[256,128]{1,0:T(8,128)S(1)}, f32[8,32,128]{2,1,0:T(8,128)S(1)}, f32[8,32,128]{2,1,0:T(8,128)S(1)}) custom-call(s32[259]{0:T(512)S(1)} %pad_add_fusion.ints, f32[257]{0:T(512)S(1)} %pad_maximum_fusion.1.floats, f32[16,32,128]{2,1,0:T(8,128)S(1)} %collective-permute-done.2.refs_0_, ...), custom_call_target="tpu_custom_call" | custom-call | tf_op jit(solution)/shard_map/both_cycles/pallas_call | solution.py:540
  27.0 1.9 %collective-permute-start.8 = (f32[8,32,128]{2,1,0:T(8,128)S(1)}, f32[8,32,128]{2,1,0:T(8,128)S(1)}, u32[]{:S(2)}, u32[]{:S(2)}) collective-permute-start(f32[8,32,128]{2,1,0:T(8,128)S(1)} %get-tuple-element.21), channel_id=1, source_target_pairs={{0,1},{1,0},{2,3},{3,2},{4,5},{5,4},{6,7},{7,6},{8,9},{9,8},{10,11... | collective-permute-start | bytes 393224 | tf_op jit(solution)/shard_map/ppermute | solution.py:557
  28.9 2.5 %collective-permute-start.10 = (f32[8,32,128]{2,1,0:T(8,128)S(1)}, f32[8,32,128]{2,1,0:T(8,128)S(1)}, u32[]{:S(2)}, u32[]{:S(2)}) collective-permute-start(f32[8,32,128]{2,1,0:T(8,128)S(1)} %get-tuple-element.22), channel_id=1, source_target_pairs={{0,3},{1,2},{2,1},{3,0},{4,7},{5,6},{6,5},{7,4},{8,11},{9,10},{10,... | collective-permute-start | bytes 393224 | tf_op jit(solution)/shard_map/ppermute | solution.py:557
  31.3 1.3 %collective-permute-done.8 = f32[8,32,128]{2,1,0:T(8,128)S(1)} collective-permute-done((f32[8,32,128]{2,1,0:T(8,128)S(1)}, f32[8,32,128]{2,1,0:T(8,128)S(1)}, u32[]{:S(2)}, u32[]{:S(2)}) %collective-permute-start.8) | collective-permute-done | bytes 131104 | tf_op jit(solution)/shard_map/ppermute | solution.py:557
  32.7 6.6 %collective-permute-start.9 = (f32[8,32,128]{2,1,0:T(8,128)S(1)}, f32[8,32,128]{2,1,0:T(8,128)S(1)}, u32[]{:S(2)}, u32[]{:S(2)}) collective-permute-start(f32[8,32,128]{2,1,0:T(8,128)S(1)} %add.12), channel_id=1, source_target_pairs={{0,3},{1,2},{2,1},{3,0},{4,7},{5,6},{6,5},{7,4},{8,11},{9,10},{10,... | collective-permute-start | bytes 393224 | tf_op jit(solution)/shard_map/ppermute | solution.py:557
  39.3 0.0 collective-permute-done.10
  39.4 0.7 %collective-permute-start.11 = (f32[8,32,128]{2,1,0:T(8,128)S(1)}, f32[8,32,128]{2,1,0:T(8,128)S(1)}, u32[]{:S(2)}, u32[]{:S(2)}) collective-permute-start(f32[8,32,128]{2,1,0:T(8,128)S(1)} %add.14), channel_id=1, source_target_pairs={{0,1},{1,0},{2,3},{3,2},{4,5},{5,4},{6,7},{7,6},{8,9},{9,8},{10,11... | collective-permute-start | bytes 393224 | tf_op jit(solution)/shard_map/ppermute | solution.py:557
  40.1 0.7 %reduce_sum.9 = f32[256]{0:T(256)} reduce(f32[256,128]{1,0:T(8,128)S(1)} %get-tuple-element.20, f32[]{:T(128)} %constant.6.clone.1), dimensions={1}, to_apply=%region_0.0 | reduce | flops 32512 | bytes 132100 | tf_op jit(solution)/shard_map/reduce_sum | solution.py:586
  40.8 2.9 %collective-permute-done.9 = f32[8,32,128]{2,1,0:T(8,128)S(1)} collective-permute-done((f32[8,32,128]{2,1,0:T(8,128)S(1)}, f32[8,32,128]{2,1,0:T(8,128)S(1)}, u32[]{:S(2)}, u32[]{:S(2)}) %collective-permute-start.9) | collective-permute-done | bytes 131104 | tf_op jit(solution)/shard_map/ppermute | solution.py:557
  43.7 1.0 %collective-permute-done.11 = f32[8,32,128]{2,1,0:T(8,128)S(1)} collective-permute-done((f32[8,32,128]{2,1,0:T(8,128)S(1)}, f32[8,32,128]{2,1,0:T(8,128)S(1)}, u32[]{:S(2)}, u32[]{:S(2)}) %collective-permute-start.11) | collective-permute-done | bytes 131104 | tf_op jit(solution)/shard_map/ppermute | solution.py:557
  44.8 0.7 %pad_maximum_fusion = f32[16,32,128]{2,1,0:T(8,128)} fusion(f32[8,32,128]{2,1,0:T(8,128)S(1)} %add.15, f32[8,32,128]{2,1,0:T(8,128)S(1)} %add.13), kind=kLoop, calls=%fused_computation | loop fusion | flops 65536 | bytes 524288 | tf_op jit(solution)/shard_map/concatenate | solution.py:595
  (8 shorter events, 0.1 us)
Async XLA Ops:
  0.6 4.9 %collective-permute-start.1 = (f32[16,32,128]{2,1,0:T(8,128)}, f32[16,32,128]{2,1,0:T(8,128)S(1)}, u32[]{:S(2)}, u32[]{:S(2)}) collective-permute-start(f32[16,32,128]{2,1,0:T(8,128)} %param.6), channel_id=1, source_target_pairs={{0,4},{4,0},{8,12},{12,8},{1,5},{5,1},{9,13},{13,9},{2,6},{6,2},{1... | collective-permute-start | bytes 786440 | tf_op jit(solution)/shard_map/ppermute | solution.py:557
  1.1 9.9 %collective-permute-start.5 = (f32[16,32,128]{2,1,0:T(8,128)}, f32[16,32,128]{2,1,0:T(8,128)S(1)}, u32[]{:S(2)}, u32[]{:S(2)}) collective-permute-start(f32[16,32,128]{2,1,0:T(8,128)} %param.6), channel_id=1, source_target_pairs={{0,8},{4,12},{8,0},{12,4},{1,9},{5,13},{9,1},{13,5},{2,10},{6,14},... | collective-permute-start | bytes 786440 | tf_op jit(solution)/shard_map/ppermute | solution.py:557
  5.3 1.6 %collective-permute-start.3 = (f32[16,2,8,128]{3,2,1,0:T(8,128)}, f32[16,2,8,128]{3,2,1,0:T(8,128)S(1)}, u32[]{:S(2)}, u32[]{:S(2)}) collective-permute-start(f32[16,2,8,128]{3,2,1,0:T(8,128)} %black_cells.1), channel_id=1, source_target_pairs={{0,4},{4,0},{8,12},{12,8},{1,5},{5,1},{9,13},{13,9},{2,6},{6,2},{1... | collective-permute-start | bytes 393224 | tf_op jit(solution)/shard_map/ppermute | solution.py:557
  5.5 8.1 %collective-permute-start.2 = (f32[16,32,128]{2,1,0:T(8,128)S(1)}, f32[16,32,128]{2,1,0:T(8,128)S(1)}, u32[]{:S(2)}, u32[]{:S(2)}) collective-permute-start(f32[16,32,128]{2,1,0:T(8,128)S(1)} %collective-permute-done.1.refs_2_), channel_id=1, source_target_pairs={{0,4},{4,0},{8,12},{12,8},{1,5},{5,1},{9,13},{13,9},{2,6},{6,2},{1... | collective-permute-start | bytes 786440 | tf_op jit(solution)/shard_map/ppermute | solution.py:557
  5.8 7.8 %collective-permute-start = (f32[16,2,8,128]{3,2,1,0:T(8,128)}, f32[16,2,8,128]{3,2,1,0:T(8,128)S(1)}, u32[]{:S(2)}, u32[]{:S(2)}) collective-permute-start(f32[16,2,8,128]{3,2,1,0:T(8,128)} %black_cells.1), channel_id=1, source_target_pairs={{0,8},{4,12},{8,0},{12,4},{1,9},{5,13},{9,1},{13,5},{2,10},{6,14},... | collective-permute-start | bytes 393224 | tf_op jit(solution)/shard_map/ppermute | solution.py:557
  6.5 4.6 %copy-start = (f32[1,256]{1,0:T(1,128)S(1)}, f32[1,256]{1,0:T(1,128)}, u32[]{:S(2)}) copy-start(f32[1,256]{1,0:T(1,128)} %param.11) | copy-start | bytes 3076
  6.9 6.7 %collective-permute-start.4 = (f32[16,2,8,128]{3,2,1,0:T(8,128)S(1)}, f32[16,2,8,128]{3,2,1,0:T(8,128)S(1)}, u32[]{:S(2)}, u32[]{:S(2)}) collective-permute-start(f32[16,2,8,128]{3,2,1,0:T(8,128)S(1)} %collective-permute-done.3.refs_6_), channel_id=1, source_target_pairs={{0,4},{4,0},{8,12},{12,8},{1,5},{5,1},{9,13},{13,9},{2,6},{6,2},{1... | collective-permute-start | bytes 393224 | tf_op jit(solution)/shard_map/ppermute | solution.py:557
  11.1 2.6 %collective-permute-start.6 = (f32[16,32,128]{2,1,0:T(8,128)S(1)}, f32[16,32,128]{2,1,0:T(8,128)S(1)}, u32[]{:S(2)}, u32[]{:S(2)}) collective-permute-start(f32[16,32,128]{2,1,0:T(8,128)S(1)} %collective-permute-done.5.refs_1_), channel_id=1, source_target_pairs={{0,4},{4,0},{8,12},{12,8},{1,5},{5,1},{9,13},{13,9},{2,6},{6,2},{1... | collective-permute-start | bytes 786440 | tf_op jit(solution)/shard_map/ppermute | solution.py:557
  11.2 0.7 %copy-start.1 = (s32[256]{0:T(256)S(1)}, s32[256]{0:T(256)}, u32[]{:S(2)}) copy-start(s32[256]{0:T(256)} %param.10) | copy-start | bytes 3076
  11.2 0.7 %copy-start.2 = (s32[1,2]{1,0:T(1,128)S(1)}, s32[1,2]{1,0:T(1,128)}, u32[]{:S(2)}) copy-start(s32[1,2]{1,0:T(1,128)} %param.8) | copy-start | bytes 28
  13.6 1.4 %collective-permute-start.7 = (f32[16,2,8,128]{3,2,1,0:T(8,128)S(1)}, f32[16,2,8,128]{3,2,1,0:T(8,128)S(1)}, u32[]{:S(2)}, u32[]{:S(2)}) collective-permute-start(f32[16,2,8,128]{3,2,1,0:T(8,128)S(1)} %collective-permute-done.refs_5_), channel_id=1, source_target_pairs={{0,4},{4,0},{8,12},{12,8},{1,5},{5,1},{9,13},{13,9},{2,6},{6,2},{1... | collective-permute-start | bytes 393224 | tf_op jit(solution)/shard_map/ppermute | solution.py:557
  27.0 5.7 %collective-permute-start.8 = (f32[8,32,128]{2,1,0:T(8,128)S(1)}, f32[8,32,128]{2,1,0:T(8,128)S(1)}, u32[]{:S(2)}, u32[]{:S(2)}) collective-permute-start(f32[8,32,128]{2,1,0:T(8,128)S(1)} %get-tuple-element.21), channel_id=1, source_target_pairs={{0,1},{1,0},{2,3},{3,2},{4,5},{5,4},{6,7},{7,6},{8,9},{9,8},{10,11... | collective-permute-start | bytes 393224 | tf_op jit(solution)/shard_map/ppermute | solution.py:557
  28.9 10.5 %collective-permute-start.10 = (f32[8,32,128]{2,1,0:T(8,128)S(1)}, f32[8,32,128]{2,1,0:T(8,128)S(1)}, u32[]{:S(2)}, u32[]{:S(2)}) collective-permute-start(f32[8,32,128]{2,1,0:T(8,128)S(1)} %get-tuple-element.22), channel_id=1, source_target_pairs={{0,3},{1,2},{2,1},{3,0},{4,7},{5,6},{6,5},{7,4},{8,11},{9,10},{10,... | collective-permute-start | bytes 393224 | tf_op jit(solution)/shard_map/ppermute | solution.py:557
  32.7 11.0 %collective-permute-start.9 = (f32[8,32,128]{2,1,0:T(8,128)S(1)}, f32[8,32,128]{2,1,0:T(8,128)S(1)}, u32[]{:S(2)}, u32[]{:S(2)}) collective-permute-start(f32[8,32,128]{2,1,0:T(8,128)S(1)} %add.12), channel_id=1, source_target_pairs={{0,3},{1,2},{2,1},{3,0},{4,7},{5,6},{6,5},{7,4},{8,11},{9,10},{10,... | collective-permute-start | bytes 393224 | tf_op jit(solution)/shard_map/ppermute | solution.py:557
  39.4 5.4 %collective-permute-start.11 = (f32[8,32,128]{2,1,0:T(8,128)S(1)}, f32[8,32,128]{2,1,0:T(8,128)S(1)}, u32[]{:S(2)}, u32[]{:S(2)}) collective-permute-start(f32[8,32,128]{2,1,0:T(8,128)S(1)} %add.14), channel_id=1, source_target_pairs={{0,1},{1,0},{2,3},{3,2},{4,5},{5,4},{6,7},{7,6},{8,9},{9,8},{10,11... | collective-permute-start | bytes 393224 | tf_op jit(solution)/shard_map/ppermute | solution.py:557

commit v5 on v4

--- a/solution.py
+++ b/solution.py
@@ -459,9 +459,9 @@
     fine_half_sweep(fine, adjoint, 0, window(2))
     fine_half_sweep(fine, adjoint, 1, window(2))
 
-    def gradient(base, out):
+    def gradient(base, out, count):
         ahead = [[fine.rows(field, base + p, p + 1) for field in (forward, adjoint)] for p in range(2)]
-        for plane in range(local // 2):
+        for plane in range(count):
             (under_p, under_a), (p, a) = ahead
             over_p, over_a = [fine.rows(field, base + plane + 2, plane + 1) for field in (forward, adjoint)]
             ahead = [(p, a), (over_p, over_a)]
@@ -489,8 +489,9 @@
                 value = value + (z_pair + z_below)
                 out[plane, pl.ds(j, SUB, stride=4), :] = -0.5 * value
 
-    gradient(first, low_out)
-    gradient(first + local // 2, high_out)
+    low_planes = low_out.shape[0]
+    gradient(first, low_out, low_planes)
+    gradient(first + low_planes, high_out, local - low_planes)
     potential_copy.wait()
 
 
@@ -533,7 +534,8 @@
         scratch += [planes(n, index) for _ in range(4)] + [planes(n + 2, index)]
     held = 4 * sum(math.prod(s.shape) for s in scratch[2:])
     held += 4 * cells_y * cells_z * local * (2 * parts + 3) + 4 * LANES * receivers
-    half = jax.ShapeDtypeStruct((local // 2, cells_y, cells_z), jnp.float32)
+    low_planes = 2 * (local * 5 // 16)
+    low, high = [jax.ShapeDtypeStruct((n, cells_y, cells_z), jnp.float32) for n in (low_planes, local - low_planes)]
     smem = pl.BlockSpec(memory_space=pltpu.SMEM)
     vmem = pl.BlockSpec(memory_space=pltpu.VMEM)
     hbm = pl.BlockSpec(memory_space=pl.ANY)
@@ -542,8 +544,8 @@
         out_shape=(
             jax.ShapeDtypeStruct((1, local, cells_y, cells_z), jnp.float32),
             jax.ShapeDtypeStruct((receivers, LANES), jnp.float32),
-            half,
-            half,
+            low,
+            high,
         ),
         in_specs=[smem] * 2 + [vmem] * (2 * parts),
         out_specs=[hbm] + [vmem] * 3,

time: 45.7 us -> 45 us (0.985)
  starting transfers between devices: 15.5 us -> 14.1 us
  waiting for transfers between devices: 12.7 us -> 13.5 us
    ppermute x12, starting transfers between devices: 15.5 us -> 14.1 us  [exchanged(): lax.ppermute(value, axis, [(i, i ^ mask) for i in range(lax.axis_size(axi...]
    ppermute x12, waiting for transfers between devices: 12.7 us -> 13.5 us  [exchanged(): lax.ppermute(value, axis, [(i, i ^ mask) for i in range(lax.axis_size(axi...]
  transfers between devices with their start and end apart: 12 -> 12, of which waited for: 7 -> 6; matrix products, arithmetic and copies ran while one was open for 2% -> 2% of each run, Pallas kernels for 4% -> 4%
where the time goes in v5:
time: 45 us; the launch traced here: 44.8 us
  starting transfers between devices  14.1 us (31%)
  Pallas kernels  13.6 us (30%)
  waiting for transfers between devices  13.5 us (30%)
  other arithmetic  1.63 us (4%)
  between operations  1.36 us (3%)
  local copies, waits for them, and re-layouts  0.69 us (2%)
    ppermute x12, starting transfers between devices, exchanged(): lax.ppermute(value, axis, [(i, i ^ mask) for i in range(lax.axis_size(axi...  14.1 us
    ppermute x12, waiting for transfers between devices, exchanged(): lax.ppermute(value, axis, [(i, i ^ mask) for i in range(lax.axis_size(axi...  13.5 us
    pallas_call x1, Pallas kernels, solve(): pl.pallas_call(functools.partial(kernel, masks, total), out_shape=(jax.Sh...  12 us
    pallas_call x1, Pallas kernels, black_cells(): pl.pallas_call(black_kernel, out_shape=jax.ShapeDtypeStruct((prior.shape[...  1.62 us
  transfers between devices with their start and end apart: 12, of which 6 were waited for; matrix products, arithmetic and copies ran while one was open for 2% of the time, Pallas kernels for 4%

profile of v5, /device:TPU:0, one launch (start us, length us, event | category | flops | bytes accessed | tf_op | source)
XLA Modules:
  0.0 44.8 jit_solution(1104371093259671123)
XLA Ops:
  0.6 0.5 %collective-permute-start.1 = (f32[16,32,128]{2,1,0:T(8,128)}, f32[16,32,128]{2,1,0:T(8,128)S(1)}, u32[]{:S(2)}, u32[]{:S(2)}) collective-permute-start(f32[16,32,128]{2,1,0:T(8,128)} %param.6), channel_id=1, source_target_pairs={{0,4},{4,0},{8,12},{12,8},{1,5},{5,1},{9,13},{13,9},{2,6},{6,2},{1... | collective-permute-start | bytes 786440 | tf_op jit(solution)/shard_map/ppermute | solution.py:559
  1.1 2.6 %collective-permute-start.5 = (f32[16,32,128]{2,1,0:T(8,128)}, f32[16,32,128]{2,1,0:T(8,128)S(1)}, u32[]{:S(2)}, u32[]{:S(2)}) collective-permute-start(f32[16,32,128]{2,1,0:T(8,128)} %param.6), channel_id=1, source_target_pairs={{0,8},{4,12},{8,0},{12,4},{1,9},{5,13},{9,1},{13,5},{2,10},{6,14},... | collective-permute-start | bytes 786440 | tf_op jit(solution)/shard_map/ppermute | solution.py:559
  3.7 1.6 %black_cells.1 = f32[16,2,8,128]{3,2,1,0:T(8,128)} custom-call(f32[1,16,32,128]{3,2,1,0:T(8,128)} %prior.1), custom_call_target="tpu_custom_call" | custom-call | tf_op jit(solution)/shard_map/black_cells/pallas_call | solution.py:508
  5.3 0.2 collective-permute-start.3
  5.5 0.0 collective-permute-done.1.refs_2_
  5.5 0.3 collective-permute-start.2
  5.8 0.0 collective-permute-start
  6.5 0.0 copy-start
  6.5 0.4 collective-permute-done.3.refs_6_
  6.9 0.2 collective-permute-start.4
  7.1 4.0 %collective-permute-done.5.refs_1_ = f32[16,32,128]{2,1,0:T(8,128)S(1)} collective-permute-done((f32[16,32,128]{2,1,0:T(8,128)}, f32[16,32,128]{2,1,0:T(8,128)S(1)}, u32[]{:S(2)}, u32[]{:S(2)}) %collective-permute-start.5) | collective-permute-done | bytes 262176 | tf_op jit(solution)/shard_map/ppermute | solution.py:559
  11.1 0.0 collective-permute-start.6
  11.1 0.1 pad_maximum_fusion.1.floats
  11.2 0.7 %copy-done.1 = s32[256]{0:T(256)S(1)} copy-done((s32[256]{0:T(256)S(1)}, s32[256]{0:T(256)}, u32[]{:S(2)}) %copy-start.1) | copy-done | bytes 1048
  11.8 0.1 pad_add_fusion.ints
  11.9 1.7 %collective-permute-done.refs_5_ = f32[16,2,8,128]{3,2,1,0:T(8,128)S(1)} collective-permute-done((f32[16,2,8,128]{3,2,1,0:T(8,128)}, f32[16,2,8,128]{3,2,1,0:T(8,128)S(1)}, u32[]{:S(2)}, u32[]{:S(2)}) %collective-permute-start) | collective-permute-done | bytes 131104 | tf_op jit(solution)/shard_map/ppermute | solution.py:559
  13.6 0.0 collective-permute-done.4.refs_4_
  13.6 0.0 collective-permute-done.2.refs_0_
  13.6 0.0 collective-permute-start.7
  13.6 0.0 collective-permute-done.6.refs_3_
  13.7 1.3 %collective-permute-done.7.refs_7_ = f32[16,2,8,128]{3,2,1,0:T(8,128)S(1)} collective-permute-done((f32[16,2,8,128]{3,2,1,0:T(8,128)S(1)}, f32[16,2,8,128]{3,2,1,0:T(8,128)S(1)}, u32[]{:S(2)}, u32[]{:S(2)}) %collective-permute-start.7) | collective-permute-done | bytes 131104 | tf_op jit(solution)/shard_map/ppermute | solution.py:559
  15.0 12.0 %both_cycles.1 = (f32[1,16,32,128]{3,2,1,0:T(8,128)}, f32[256,128]{1,0:T(8,128)S(1)}, f32[10,32,128]{2,1,0:T(8,128)S(1)}, f32[6,32,128]{2,1,0:T(8,128)S(1)}) custom-call(s32[259]{0:T(512)S(1)} %pad_add_fusion.ints, f32[257]{0:T(512)S(1)} %pad_maximum_fusion.1.floats, f32[16,32,128]{2,1,0:T(8,128)S(1)} %collective-permute-done.2.refs_0_, ...), custom_call_target="tpu_custom_call" | custom-call | tf_op jit(solution)/shard_map/both_cycles/pallas_call | solution.py:542
  27.0 1.9 %collective-permute-start.8 = (f32[10,32,128]{2,1,0:T(8,128)S(1)}, f32[10,32,128]{2,1,0:T(8,128)S(1)}, u32[]{:S(2)}, u32[]{:S(2)}) collective-permute-start(f32[10,32,128]{2,1,0:T(8,128)S(1)} %get-tuple-element.21), channel_id=1, source_target_pairs={{0,1},{1,0},{2,3},{3,2},{4,5},{5,4},{6,7},{7,6},{8,9},{9,8},{10,11... | collective-permute-start | bytes 491528 | tf_op jit(solution)/shard_map/ppermute | solution.py:559
  28.9 2.5 %collective-permute-start.10 = (f32[6,32,128]{2,1,0:T(8,128)S(1)}, f32[6,32,128]{2,1,0:T(8,128)S(1)}, u32[]{:S(2)}, u32[]{:S(2)}) collective-permute-start(f32[6,32,128]{2,1,0:T(8,128)S(1)} %get-tuple-element.22), channel_id=1, source_target_pairs={{0,3},{1,2},{2,1},{3,0},{4,7},{5,6},{6,5},{7,4},{8,11},{9,10},{10,... | collective-permute-start | bytes 294920 | tf_op jit(solution)/shard_map/ppermute | solution.py:559
  31.4 2.1 %collective-permute-done.8 = f32[10,32,128]{2,1,0:T(8,128)S(1)} collective-permute-done((f32[10,32,128]{2,1,0:T(8,128)S(1)}, f32[10,32,128]{2,1,0:T(8,128)S(1)}, u32[]{:S(2)}, u32[]{:S(2)}) %collective-permute-start.8) | collective-permute-done | bytes 163872 | tf_op jit(solution)/shard_map/ppermute | solution.py:559
  33.5 5.9 %collective-permute-start.9 = (f32[10,32,128]{2,1,0:T(8,128)S(1)}, f32[10,32,128]{2,1,0:T(8,128)S(1)}, u32[]{:S(2)}, u32[]{:S(2)}) collective-permute-start(f32[10,32,128]{2,1,0:T(8,128)S(1)} %add.12), channel_id=1, source_target_pairs={{0,3},{1,2},{2,1},{3,0},{4,7},{5,6},{6,5},{7,4},{8,11},{9,10},{10,... | collective-permute-start | bytes 491528 | tf_op jit(solution)/shard_map/ppermute | solution.py:559
  39.4 0.0 collective-permute-done.10
  39.4 0.1 collective-permute-start.11
  39.5 0.7 %reduce_sum.9 = f32[256]{0:T(256)} reduce(f32[256,128]{1,0:T(8,128)S(1)} %get-tuple-element.20, f32[]{:T(128)} %constant.6.clone.1), dimensions={1}, to_apply=%region_0.0 | reduce | flops 32512 | bytes 132100 | tf_op jit(solution)/shard_map/reduce_sum | solution.py:588
  40.1 3.9 %collective-permute-done.11 = f32[6,32,128]{2,1,0:T(8,128)S(1)} collective-permute-done((f32[6,32,128]{2,1,0:T(8,128)S(1)}, f32[6,32,128]{2,1,0:T(8,128)S(1)}, u32[]{:S(2)}, u32[]{:S(2)}) %collective-permute-start.11) | collective-permute-done | bytes 98336 | tf_op jit(solution)/shard_map/ppermute | solution.py:559
  44.1 0.0 collective-permute-done.9
  44.1 0.7 %pad_maximum_fusion = f32[16,32,128]{2,1,0:T(8,128)} fusion(f32[6,32,128]{2,1,0:T(8,128)S(1)} %add.15, f32[10,32,128]{2,1,0:T(8,128)S(1)} %add.13), kind=kLoop, calls=%fused_computation | loop fusion | flops 65536 | bytes 524288 | tf_op jit(solution)/shard_map/concatenate | solution.py:597
  (8 shorter events, 0.1 us)
Async XLA Ops:
  0.6 4.9 %collective-permute-start.1 = (f32[16,32,128]{2,1,0:T(8,128)}, f32[16,32,128]{2,1,0:T(8,128)S(1)}, u32[]{:S(2)}, u32[]{:S(2)}) collective-permute-start(f32[16,32,128]{2,1,0:T(8,128)} %param.6), channel_id=1, source_target_pairs={{0,4},{4,0},{8,12},{12,8},{1,5},{5,1},{9,13},{13,9},{2,6},{6,2},{1... | collective-permute-start | bytes 786440 | tf_op jit(solution)/shard_map/ppermute | solution.py:559
  1.1 9.9 %collective-permute-start.5 = (f32[16,32,128]{2,1,0:T(8,128)}, f32[16,32,128]{2,1,0:T(8,128)S(1)}, u32[]{:S(2)}, u32[]{:S(2)}) collective-permute-start(f32[16,32,128]{2,1,0:T(8,128)} %param.6), channel_id=1, source_target_pairs={{0,8},{4,12},{8,0},{12,4},{1,9},{5,13},{9,1},{13,5},{2,10},{6,14},... | collective-permute-start | bytes 786440 | tf_op jit(solution)/shard_map/ppermute | solution.py:559
  5.3 1.6 %collective-permute-start.3 = (f32[16,2,8,128]{3,2,1,0:T(8,128)}, f32[16,2,8,128]{3,2,1,0:T(8,128)S(1)}, u32[]{:S(2)}, u32[]{:S(2)}) collective-permute-start(f32[16,2,8,128]{3,2,1,0:T(8,128)} %black_cells.1), channel_id=1, source_target_pairs={{0,4},{4,0},{8,12},{12,8},{1,5},{5,1},{9,13},{13,9},{2,6},{6,2},{1... | collective-permute-start | bytes 393224 | tf_op jit(solution)/shard_map/ppermute | solution.py:559
  5.5 8.1 %collective-permute-start.2 = (f32[16,32,128]{2,1,0:T(8,128)S(1)}, f32[16,32,128]{2,1,0:T(8,128)S(1)}, u32[]{:S(2)}, u32[]{:S(2)}) collective-permute-start(f32[16,32,128]{2,1,0:T(8,128)S(1)} %collective-permute-done.1.refs_2_), channel_id=1, source_target_pairs={{0,4},{4,0},{8,12},{12,8},{1,5},{5,1},{9,13},{13,9},{2,6},{6,2},{1... | collective-permute-start | bytes 786440 | tf_op jit(solution)/shard_map/ppermute | solution.py:559
  5.8 7.8 %collective-permute-start = (f32[16,2,8,128]{3,2,1,0:T(8,128)}, f32[16,2,8,128]{3,2,1,0:T(8,128)S(1)}, u32[]{:S(2)}, u32[]{:S(2)}) collective-permute-start(f32[16,2,8,128]{3,2,1,0:T(8,128)} %black_cells.1), channel_id=1, source_target_pairs={{0,8},{4,12},{8,0},{12,4},{1,9},{5,13},{9,1},{13,5},{2,10},{6,14},... | collective-permute-start | bytes 393224 | tf_op jit(solution)/shard_map/ppermute | solution.py:559
  6.5 4.6 %copy-start = (f32[1,256]{1,0:T(1,128)S(1)}, f32[1,256]{1,0:T(1,128)}, u32[]{:S(2)}) copy-start(f32[1,256]{1,0:T(1,128)} %param.11) | copy-start | bytes 3076
  6.9 6.7 %collective-permute-start.4 = (f32[16,2,8,128]{3,2,1,0:T(8,128)S(1)}, f32[16,2,8,128]{3,2,1,0:T(8,128)S(1)}, u32[]{:S(2)}, u32[]{:S(2)}) collective-permute-start(f32[16,2,8,128]{3,2,1,0:T(8,128)S(1)} %collective-permute-done.3.refs_6_), channel_id=1, source_target_pairs={{0,4},{4,0},{8,12},{12,8},{1,5},{5,1},{9,13},{13,9},{2,6},{6,2},{1... | collective-permute-start | bytes 393224 | tf_op jit(solution)/shard_map/ppermute | solution.py:559
  11.1 2.6 %collective-permute-start.6 = (f32[16,32,128]{2,1,0:T(8,128)S(1)}, f32[16,32,128]{2,1,0:T(8,128)S(1)}, u32[]{:S(2)}, u32[]{:S(2)}) collective-permute-start(f32[16,32,128]{2,1,0:T(8,128)S(1)} %collective-permute-done.5.refs_1_), channel_id=1, source_target_pairs={{0,4},{4,0},{8,12},{12,8},{1,5},{5,1},{9,13},{13,9},{2,6},{6,2},{1... | collective-permute-start | bytes 786440 | tf_op jit(solution)/shard_map/ppermute | solution.py:559
  11.2 0.7 %copy-start.1 = (s32[256]{0:T(256)S(1)}, s32[256]{0:T(256)}, u32[]{:S(2)}) copy-start(s32[256]{0:T(256)} %param.10) | copy-start | bytes 3076
  11.2 0.7 %copy-start.2 = (s32[1,2]{1,0:T(1,128)S(1)}, s32[1,2]{1,0:T(1,128)}, u32[]{:S(2)}) copy-start(s32[1,2]{1,0:T(1,128)} %param.8) | copy-start | bytes 28
  13.6 1.4 %collective-permute-start.7 = (f32[16,2,8,128]{3,2,1,0:T(8,128)S(1)}, f32[16,2,8,128]{3,2,1,0:T(8,128)S(1)}, u32[]{:S(2)}, u32[]{:S(2)}) collective-permute-start(f32[16,2,8,128]{3,2,1,0:T(8,128)S(1)} %collective-permute-done.refs_5_), channel_id=1, source_target_pairs={{0,4},{4,0},{8,12},{12,8},{1,5},{5,1},{9,13},{13,9},{2,6},{6,2},{1... | collective-permute-start | bytes 393224 | tf_op jit(solution)/shard_map/ppermute | solution.py:559
  27.0 6.5 %collective-permute-start.8 = (f32[10,32,128]{2,1,0:T(8,128)S(1)}, f32[10,32,128]{2,1,0:T(8,128)S(1)}, u32[]{:S(2)}, u32[]{:S(2)}) collective-permute-start(f32[10,32,128]{2,1,0:T(8,128)S(1)} %get-tuple-element.21), channel_id=1, source_target_pairs={{0,1},{1,0},{2,3},{3,2},{4,5},{5,4},{6,7},{7,6},{8,9},{9,8},{10,11... | collective-permute-start | bytes 491528 | tf_op jit(solution)/shard_map/ppermute | solution.py:559
  28.9 10.5 %collective-permute-start.10 = (f32[6,32,128]{2,1,0:T(8,128)S(1)}, f32[6,32,128]{2,1,0:T(8,128)S(1)}, u32[]{:S(2)}, u32[]{:S(2)}) collective-permute-start(f32[6,32,128]{2,1,0:T(8,128)S(1)} %get-tuple-element.22), channel_id=1, source_target_pairs={{0,3},{1,2},{2,1},{3,0},{4,7},{5,6},{6,5},{7,4},{8,11},{9,10},{10,... | collective-permute-start | bytes 294920 | tf_op jit(solution)/shard_map/ppermute | solution.py:559
  33.5 10.6 %collective-permute-start.9 = (f32[10,32,128]{2,1,0:T(8,128)S(1)}, f32[10,32,128]{2,1,0:T(8,128)S(1)}, u32[]{:S(2)}, u32[]{:S(2)}) collective-permute-start(f32[10,32,128]{2,1,0:T(8,128)S(1)} %add.12), channel_id=1, source_target_pairs={{0,3},{1,2},{2,1},{3,0},{4,7},{5,6},{6,5},{7,4},{8,11},{9,10},{10,... | collective-permute-start | bytes 491528 | tf_op jit(solution)/shard_map/ppermute | solution.py:559
  39.4 4.7 %collective-permute-start.11 = (f32[6,32,128]{2,1,0:T(8,128)S(1)}, f32[6,32,128]{2,1,0:T(8,128)S(1)}, u32[]{:S(2)}, u32[]{:S(2)}) collective-permute-start(f32[6,32,128]{2,1,0:T(8,128)S(1)} %add.14), channel_id=1, source_target_pairs={{0,1},{1,0},{2,3},{3,2},{4,5},{5,4},{6,7},{7,6},{8,9},{9,8},{10,11... | collective-permute-start | bytes 294920 | tf_op jit(solution)/shard_map/ppermute | solution.py:559
